TPU v7x, 512 devices: a whole 4x8x8 slice. The times are simulated.
512 devices in a mesh: section: 8 (over z_lo, core), tensor: 8 (over y), copy: 8 (over x, z_hi).
Axes of the slice: x: 4, y: 8, z: 8 (z_hi: 2, z_lo: 4; z = z_hi * 4 + z_lo), core: 2. Of those that a mesh axis runs over, the one named last changes fastest.
Arguments:
- visual: bfloat16 [8, 192, 8192], P('copy', ('section', 'tensor')), may hold values from -6 to 6
- w_key: bfloat16 [8, 8192, 1024], P('section', None, 'tensor'), may hold values from -0.0625 to 0.0625
- w_value: bfloat16 [8, 8192, 1024], P('section', None, 'tensor'), may hold values from -0.0625 to 0.0625
- key_gain: bfloat16 [8, 1024], P('section', 'tensor'), may hold values from 0.25 to 1.75
- queries: bfloat16 [8, 8, 128, 8192], P('section', 'copy', None, 'tensor')
- grad_out: bfloat16 [8, 8, 128, 8192], P('section', 'copy', None, 'tensor'), may hold values from -6 to 6
- offsets: int32 [8], P('copy'), may hold values from 0 to 8
- flips: int32 [8], P('copy'), may hold values from 0 to 1
- lengths: int32 [8], P('copy'), may hold values from 32 to 128, as said below
Outputs:
- patch_grad: float32 [256, 8192], P('section', 'tensor')
Inputs may be any that keep to these rules, and one draw needn't show every extreme that they name: `lengths`: every length is at least a quarter of 128, and some copy has all 128 tokens live.
All inputs are finite; a program needn't handle non-finite values.
Results may differ from a plain program's by a relative error of at most 0.014.
The roundings to bfloat16 on the way count: a program that leaves them out, or rounds other values in their place, can miss the bound.
Values may be sent and summed in bfloat16 or wider, within the bound.
No kernel may reach another device: no remote copies, remote signals or barrier semaphores. Data moves between devices by JAX's collectives and lax.ppermute only.
A program may use at most 64 MiB of HBM per device.

v0:
```python
import jax
import jax.numpy as jnp
from jax import lax
from jax.sharding import PartitionSpec as P

GW = 24
BW = 32


EPS = 1e-05


def place_patches(grid, offset, flip):
    column = jnp.arange(GW, dtype=jnp.int32)
    target = offset + jnp.where(flip == 1, GW - 1 - column, column)
    onehot = (jnp.arange(BW, dtype=jnp.int32)[:, None] == target[None, :]).astype(jnp.float32)
    return jnp.einsum("bj,rjd->rbd", onehot, grid, precision=lax.Precision.HIGHEST)


def on_device(visual, w_key, w_value, key_gain, queries, grad_out, offsets, flips, lengths):
    key_mat = w_key[0]
    value_mat = w_value[0]
    head_size = key_mat.shape[1]
    rows = lax.all_gather(visual, ("section", "tensor"), axis=1, tiled=True)[0]
    kraw = jnp.dot(rows, key_mat, preferred_element_type=jnp.float32)
    vraw = jnp.dot(rows, value_mat, preferred_element_type=jnp.float32)
    both = jnp.concatenate([kraw, vraw], axis=1)
    kraw = both[:, :head_size]
    values = both[:, head_size:].astype(jnp.bfloat16)
    gain = key_gain[0].astype(jnp.float32)

    def normed_keys(raw):
        scale_row = lax.rsqrt(jnp.mean(raw * raw, axis=-1, keepdims=True) + EPS)
        return raw * scale_row * gain

    normed, pull = jax.vjp(normed_keys, kraw)
    keys = normed.astype(jnp.bfloat16)
    text_len = queries.shape[2]
    query = queries[0, 0].reshape(text_len, -1, head_size)
    scale = head_size ** (-0.5)
    live = (jnp.arange(text_len, dtype=jnp.int32) < lengths[0]).astype(jnp.bfloat16)
    dout = (grad_out[0, 0] * live[:, None]).reshape(text_len, -1, head_size)
    scores = jnp.einsum("tgd,vd->gtv", query, keys, preferred_element_type=jnp.float32) * scale
    probs = jax.nn.softmax(scores, axis=-1)
    weights = probs.astype(jnp.bfloat16)
    dval = jnp.einsum("gtv,tgd->vd", weights, dout, preferred_element_type=jnp.float32)
    dprob = jnp.einsum("tgd,vd->gtv", dout, values, preferred_element_type=jnp.float32)
    dscore = probs * (dprob - jnp.sum(probs * dprob, axis=-1, keepdims=True)) * scale
    dkey = jnp.einsum(
        "gtv,tgd->vd", dscore.astype(jnp.bfloat16), query, preferred_element_type=jnp.float32
    )
    (dkraw,) = pull(dkey)
    term = jnp.einsum(
        "vk,dk->vd", dkraw.astype(jnp.bfloat16), key_mat, preferred_element_type=jnp.float32
    )
    term = term + jnp.einsum(
        "vk,dk->vd", dval.astype(jnp.bfloat16), value_mat, preferred_element_type=jnp.float32
    )
    term = term.astype(jnp.bfloat16).astype(jnp.float32)
    summed = lax.psum_scatter(
        term.astype(jnp.bfloat16), "tensor", scatter_dimension=1, tiled=True
    ).astype(jnp.float32)
    width = summed.shape[1]
    owned = lax.psum_scatter(summed, "section", scatter_dimension=0, tiled=True)
    placed = place_patches(owned.reshape(-1, GW, width), offsets[0], flips[0]).reshape(-1, width)
    result = lax.psum(placed, "copy")
    return result


def solution(mesh):
    placed = (
        P("copy", ("section", "tensor"), None),
        P("section", None, "tensor"),
        P("section", None, "tensor"),
        P("section", "tensor"),
        P("section", "copy", None, "tensor"),
        P("section", "copy", None, "tensor"),
        P("copy"),
        P("copy"),
        P("copy"),
    )
    return jax.shard_map(
        on_device, mesh=mesh, in_specs=placed, out_specs=P("section", "tensor"), check_vma=False
    )
```

profile of v0, /device:TPU:1, one launch (start us, length us, event | category | flops | bytes accessed | tf_op | source)
XLA Modules:
  0.0 449.4 jit_solution(14312060028936896208)
XLA Ops:
  6.5 0.0 copy-start
  6.5 0.0 all-gather.2.cloned.1.call-start
  6.5 1.7 copy.17
  8.3 0.0 all-gather.2.cloned.1.call-update
  8.3 0.0 reduce-scatter.3.cloned.1.call-start
  8.3 1.0 copy.22
  9.3 1.0 copy.23
  11.0 0.7 bitcast_convert_fusion
  11.7 197.1 %all-gather.2.cloned.1.call-done = bf16[1,192,8192]{2,0,1:T(2,128)(2,1)} async-done(((bf16[1,3,8192]{2,0,1:T(2,128)(2,1)}), bf16[1,192,8192]{2,0,1:T(2,128)(2,1)}) %all-gather.2.cloned.1.call-update) | async-done | bytes 3145744 | tf_op jit(solution)/shard_map/all_gather | solution.py:24
  208.7 7.2 %multiply_reduce_fusion.2 = (f32[192]{0:T(256)S(1)}, f32[192,128]{1,0:T(8,128)S(1)}) fusion(bf16[1,8192,128]{2,1,0:T(8,128)(2,1)} %param.10, bf16[1,192,8192]{2,0,1:T(2,128)(2,1)} %all-gather.2.cloned.1.call-done), kind=kOutput, calls=%fused_computation.46 | convolution fusion | flops 402702144 | bytes 5341952 | tf_op jit(solution)/shard_map/dot_general | solution.py:25
  215.9 0.5 fusion.70
  216.4 0.0 copy-done
  216.4 7.5 %convolution_bitcast_fusion = f32[8,128,192]{1,2,0:T(8,128)} fusion(bf16[1,8192,128]{2,1,0:T(8,128)(2,1)S(1)} %copy-done, bf16[1,192,8192]{2,0,1:T(2,128)(2,1)} %all-gather.2.cloned.1.call-done, bf16[128,8,128]{2,1,0:T(8,128)(2,1)S(1)} %bitcast.87, bf16[128]{0:T(256)(128)(2,1)S(1)} %compare_convert_fusion), kind=kOutput, calls=%fused_computation.18 | convolution fusion | flops 453533696 | bytes 6291712 | tf_op jit(solution)/shard_map/tgd,vd->gtv/dot_general | solution.py:47
  223.9 2.4 multiply_reduce_fusion.1
  226.3 5.3 %fusion.9 = f32[192,8192]{1,0:T(8,128)} fusion(bf16[1,8192,128]{2,1,0:T(8,128)(2,1)} %param.10, f32[192,128]{1,0:T(8,128)S(1)} %get-tuple-element.6, f32[192,128]{1,0:T(8,128)} %get-tuple-element.10, f32[192]{0:T(256)S(1)} %multiply_multiply_fusion, f32[192]{0:T(256)S(1)} %fusion.57), kind=kOutput, calls=%fused_computation.10 | convolution fusion | flops 402776064 | bytes 8586752 | tf_op jit(solution)/shard_map/vk,dk->vd/dot_general | solution.py:53
  231.6 5.7 %fusion.2 = bf16[192,8192]{1,0:T(8,128)(2,1)} fusion(f32[192,8192]{1,0:T(8,128)} %fusion.9, bf16[1,8192,128]{2,1,0:T(8,128)(2,1)S(1)} %copy-done, bf16[128,8,128]{2,1,0:T(8,128)(2,1)S(1)} %bitcast.88, bf16[128]{0:T(256)(128)(2,1)S(1)} %compare_convert_fusion, f32[8,128,192]{1,2,0:T(8,128)S(1)} %get-tuple-element.8, f32[8,128]{1,0:T(8,128)S(1)} %get-tuple-element.7), kind=kOutput, calls=%fused_computation.3 | convolution fusion | flops 456679424 | bytes 12587264 | tf_op jit(solution)/shard_map/vk,dk->vd/dot_general | solution.py:56
  237.3 0.0 reduce-scatter.3.cloned.1.call-update
  237.4 0.0 reduce-scatter.5.cloned.1.call-start
  237.4 49.1 %reduce-scatter.3.cloned.1.call-done = bf16[192,1024]{1,0:T(8,128)(2,1)} async-done(((bf16[192,8192]{1,0:T(8,128)(2,1)}), bf16[192,1024]{1,0:T(8,128)(2,1)}) %reduce-scatter.3.cloned.1.call-update) | async-done | bytes 393232 | tf_op jit(solution)/shard_map/reduce_scatter | solution.py:60
  286.5 2.0 convert_element_type.44
  288.5 0.0 reduce-scatter.5.cloned.1.call-update
  288.5 0.0 all-reduce.2.cloned.1.call-start
  289.9 40.2 %reduce-scatter.5.cloned.1.call-done = f32[24,1024]{1,0:T(8,128)} async-done(((f32[192,1024]{1,0:T(8,128)}), f32[24,1024]{1,0:T(8,128)}) %reduce-scatter.5.cloned.1.call-update) | async-done | bytes 98320 | tf_op jit(solution)/shard_map/reduce_scatter | solution.py:64
  330.0 1.7 convolution_bitcast_fusion.1
  331.8 0.0 all-reduce.2.cloned.1.call-update
  331.8 109.5 %all-reduce.2.cloned.1.call-done = f32[32,1024]{1,0:T(8,128)} async-done(((f32[32,1024]{1,0:T(8,128)}), f32[32,1024]{1,0:T(8,128)}) %all-reduce.2.cloned.1.call-update) | async-done | bytes 131088 | tf_op jit(solution)/shard_map/psum | solution.py:66
  441.3 1.6 copy.60
  (4 shorter events, 0.0 us)
Async XLA Ops:
  6.5 209.9 %copy-start = (bf16[1,8192,128]{2,1,0:T(8,128)(2,1)S(1)}, bf16[1,8192,128]{2,1,0:T(8,128)(2,1)}, u32[]{:S(2)}) copy-start(bf16[1,8192,128]{2,1,0:T(8,128)(2,1)} %param.11) | copy-start | bytes 6291460
  6.5 202.2 %all-gather.2.cloned.1.call-start = ((), (), s32[]{:S(2)}) async-start(), calls=%async_computation.2 | async-start | bytes 6389760 | tf_op jit(solution)/shard_map/all_gather | solution.py:24
  8.3 278.2 %reduce-scatter.3.cloned.1.call-start = ((), (), s32[]{:S(2)}) async-start(), calls=%async_computation.3 | async-start | bytes 3538944 | tf_op jit(solution)/shard_map/reduce_scatter | solution.py:60
  237.4 92.7 %reduce-scatter.5.cloned.1.call-start = ((), (), s32[]{:S(2)}) async-start(), calls=%async_computation.4 | async-start | bytes 884736 | tf_op jit(solution)/shard_map/reduce_scatter | solution.py:64
  288.5 152.8 %all-reduce.2.cloned.1.call-start = ((), (), s32[]{:S(2)}) async-start(), calls=%async_computation.5 | async-start | bytes 262144 | tf_op jit(solution)/shard_map/psum | solution.py:66
Sparse Core Ops, SparseCore 0:
  9.4 199.2 all-gather.1
  237.5 48.9 reduce-scatter.2
  289.4 40.6 reduce-scatter.4
  332.8 108.4 all-reduce.1
where the time goes:
time: 454 us; the launch traced here: 449 us
  waiting for transfers between devices  396 us (87%)
  matrix products  30.3 us (7%)
  between operations  15.1 us (3%)
  local copies, waits for them, and re-layouts  5.27 us (1%)
    all_gather x1, waiting for transfers between devices, on_device(): rows = lax.all_gather(visual, ('section', 'tensor'), axis=1, tiled=True)[0]  197 us
    psum x1, waiting for transfers between devices, on_device(): result = lax.psum(placed, 'copy')  109 us
    reduce_scatter x1, waiting for transfers between devices, on_device(): lax.psum_scatter(term.astype(jnp.bfloat16), 'tensor', scatter_dimension=1...  49.1 us
    reduce_scatter x1, waiting for transfers between devices, on_device(): owned = lax.psum_scatter(summed, 'section', scatter_dimension=0, tiled=True)  40.2 us
  transfers between devices with their start and end apart: 4, of which 4 were waited for; matrix products, arithmetic and copies ran while one was open for 1% of the time, Pallas kernels for 0%

commit v1 on v0

v1 whole, which is shorter than its diff:
```python
import jax
import jax.numpy as jnp
from jax import lax
from jax.sharding import Mesh, PartitionSpec as P

GW = 24
BW = 32
EPS = 1e-05
SECTION = ("zl", "core")
TENSOR = ("yh", "yl")
COPY = ("x", "zh")


def gather_rows(visual):
    shard = visual[0].reshape(1, 24, 1024)
    spread = jnp.broadcast_to(shard, (16, 24, 1024))
    same = lax.all_to_all(spread, ("zl", "yh"), 0, 0)
    same = same.reshape(48, 8192)
    up = [(y, (y + 1) % 8) for y in range(8)]
    down = [(y, (y - 1) % 8) for y in range(8)]
    low = lax.ppermute(same[:24], TENSOR, up)
    high = lax.ppermute(same[24:], TENSOR, down)
    swap = [(0, 1), (1, 0)]
    own = jnp.concatenate([same, low, high], axis=0)
    rows = jnp.concatenate([own, lax.ppermute(own, "core", swap)], axis=0)
    r = jnp.arange(192, dtype=jnp.int32)
    core = (lax.axis_index("core") + r // 96) % 2
    parity = (lax.axis_index("yl") + (r // 48) % 2) % 2
    zl = (r // 12) % 4
    yh = (r // 3) % 4
    line = zl * 2 + core
    column = (yh * 2 + parity) * 3 + r % 3
    return rows, line, column


def on_device(visual, w_key, w_value, key_gain, queries, grad_out, offsets, flips, lengths):
    key_mat = w_key[0]
    value_mat = w_value[0]
    head_size = key_mat.shape[1]
    rows, line, column = gather_rows(visual)
    kraw = jnp.dot(rows, key_mat, preferred_element_type=jnp.float32)
    vraw = jnp.dot(rows, value_mat, preferred_element_type=jnp.float32)
    values = vraw.astype(jnp.bfloat16)
    gain = key_gain[0].astype(jnp.float32)

    def normed_keys(raw):
        scale_row = lax.rsqrt(jnp.mean(raw * raw, axis=-1, keepdims=True) + EPS)
        return raw * scale_row * gain

    normed, pull = jax.vjp(normed_keys, kraw)
    keys = normed.astype(jnp.bfloat16)
    text_len = queries.shape[2]
    query = queries[0, 0].reshape(text_len, -1, head_size)
    scale = head_size ** (-0.5)
    live = (jnp.arange(text_len, dtype=jnp.int32) < lengths[0]).astype(jnp.bfloat16)
    dout = (grad_out[0, 0] * live[:, None]).reshape(text_len, -1, head_size)
    scores = jnp.einsum("tgd,vd->gtv", query, keys, preferred_element_type=jnp.float32) * scale
    probs = jax.nn.softmax(scores, axis=-1)
    weights = probs.astype(jnp.bfloat16)
    dval = jnp.einsum("gtv,tgd->vd", weights, dout, preferred_element_type=jnp.float32)
    dprob = jnp.einsum("tgd,vd->gtv", dout, values, preferred_element_type=jnp.float32)
    dscore = probs * (dprob - jnp.sum(probs * dprob, axis=-1, keepdims=True)) * scale
    dkey = jnp.einsum(
        "gtv,tgd->vd", dscore.astype(jnp.bfloat16), query, preferred_element_type=jnp.float32
    )
    (dkraw,) = pull(dkey)
    fac = jnp.concatenate([dkraw, dval], axis=1).astype(jnp.bfloat16)
    target = line * BW + offsets[0] + jnp.where(flips[0] == 1, GW - 1 - column, column)
    onehot = (jnp.arange(8 * BW, dtype=jnp.int32)[:, None] == target[None, :]).astype(jnp.bfloat16)
    placed = jnp.dot(onehot, fac, preferred_element_type=jnp.float32).astype(jnp.bfloat16)
    parts = lax.all_to_all(placed.reshape(8, BW, -1), COPY, 0, 0)
    summed = jnp.sum(parts.astype(jnp.float32), axis=0).astype(jnp.bfloat16)
    part = jnp.einsum("bk,dk->bd", summed[:, :head_size], key_mat, preferred_element_type=jnp.float32)
    part = part + jnp.einsum("bk,dk->bd", summed[:, head_size:], value_mat, preferred_element_type=jnp.float32)
    part = part.astype(jnp.bfloat16)
    cut = part.reshape(BW, 8, 4, 2, 128).transpose(3, 2, 1, 0, 4).reshape(2, 32, BW, 128)
    mine = lax.axis_index("core")
    keep = lax.dynamic_index_in_dim(cut, mine, 0, keepdims=False)
    give = lax.dynamic_index_in_dim(cut, 1 - mine, 0, keepdims=False)
    got = lax.ppermute(give, "core", [(0, 1), (1, 0)])
    pair = (keep.astype(jnp.float32) + got.astype(jnp.float32)).astype(jnp.bfloat16)
    pieces = lax.all_to_all(pair, ("zl", "yh", "yl"), 0, 0)
    total = jnp.sum(pieces.astype(jnp.float32), axis=0).astype(jnp.bfloat16)
    wide = lax.all_to_all(jnp.broadcast_to(total[None], (8, BW, 128)), SECTION, 0, 0)
    turn = [(s * 8 + c, c * 8 + s) for s in range(8) for c in range(8)]
    out = lax.ppermute(wide, SECTION + COPY, turn)
    return out.transpose(1, 0, 2).reshape(BW, 1024).astype(jnp.float32)


def solution(mesh):
    fine = Mesh(mesh.devices.reshape(4, 2, 4, 2, 4, 2), ("zl", "core", "yh", "yl", "x", "zh"))
    placed = (
        P(COPY, SECTION + TENSOR, None),
        P(SECTION, None, TENSOR),
        P(SECTION, None, TENSOR),
        P(SECTION, TENSOR),
        P(SECTION, COPY, None, TENSOR),
        P(SECTION, COPY, None, TENSOR),
        P(COPY),
        P(COPY),
        P(COPY),
    )
    return jax.shard_map(
        on_device, mesh=fine, in_specs=placed, out_specs=P(SECTION, TENSOR), check_vma=False
    )
```

time: 454 us -> 143 us (0.31)
  waiting for transfers between devices: 396 us -> 42.1 us
  starting transfers between devices: 0.13 us -> 41.5 us
  blocking collectives: 0 us -> 28.7 us
  matrix products: 30.3 us -> 12.7 us
  between operations: 15.1 us -> 2.19 us
  local copies, waits for them, and re-layouts: 5.27 us -> 12.3 us
    all_gather x1 -> x0, waiting for transfers between devices: 197 us -> none  [on_device(): rows = lax.all_gather(visual, ('section', 'tensor'), axis=1, tiled=True)[0]]
    psum x1 -> x0, waiting for transfers between devices: 109 us -> none  [on_device(): result = lax.psum(placed, 'copy')]
    reduce_scatter x2 -> x0, waiting for transfers between devices: 89.3 us -> none  [the longest x1 49.1 us: on_device(): lax.psum_scatter(term.astype(jnp.bfloat16), 'tensor', scatter_dimension=1...]
    all_to_all x0 -> x2, blocking collectives: none -> 28.7 us  [the longest x1 17.7 us: on_device(): pieces = lax.all_to_all(pair, ('zl', 'yh', 'yl'), 0, 0)]
    all_to_all x0 -> x2, waiting for transfers between devices: none -> 28.1 us  [the longest x1 18.6 us: gather_rows(): same = lax.all_to_all(spread, ('zl', 'yh'), 0, 0)]
    all_to_all x0 -> x2, starting transfers between devices: none -> 22.9 us  [the longest x1 13.2 us: gather_rows(): same = lax.all_to_all(spread, ('zl', 'yh'), 0, 0)]
    ppermute x0 -> x5, starting transfers between devices: none -> 18.6 us  [the longest x1 5.33 us: gather_rows(): rows = jnp.concatenate([own, lax.ppermute(own, 'core', swap)], axis=0)]
    ppermute x0 -> x5, waiting for transfers between devices: none -> 14 us  [the longest x1 6.44 us: on_device(): out = lax.ppermute(wide, SECTION + COPY, turn)]
  transfers between devices with their start and end apart: 4 -> 7, of which waited for: 4 -> 6; matrix products, arithmetic and copies ran while one was open for 1% -> 5% of each run, Pallas kernels for 0% -> 0%
where the time goes in v1:
time: 143 us; the launch traced here: 142 us
  waiting for transfers between devices  42.1 us (29%)
  starting transfers between devices  41.5 us (29%)
  blocking collectives  28.7 us (20%)
  matrix products  12.7 us (9%)
  local copies, waits for them, and re-layouts  12.3 us (9%)
  other arithmetic  2.87 us (2%)
  between operations  2.19 us (2%)
    all_to_all x1, waiting for transfers between devices, gather_rows(): same = lax.all_to_all(spread, ('zl', 'yh'), 0, 0)  18.6 us
    all_to_all x1, blocking collectives, on_device(): pieces = lax.all_to_all(pair, ('zl', 'yh', 'yl'), 0, 0)  17.7 us
    all_to_all x1, starting transfers between devices, gather_rows(): same = lax.all_to_all(spread, ('zl', 'yh'), 0, 0)  13.2 us
    all_to_all x1, blocking collectives, on_device(): lax.all_to_all(jnp.broadcast_to(total[None], (8, BW, 128)), SECTION, 0, 0)  11 us
    all_to_all x1, starting transfers between devices, on_device(): parts = lax.all_to_all(placed.reshape(8, BW, -1), COPY, 0, 0)  9.76 us
    all_to_all x1, waiting for transfers between devices, on_device(): parts = lax.all_to_all(placed.reshape(8, BW, -1), COPY, 0, 0)  9.46 us
    ppermute x1, waiting for transfers between devices, on_device(): out = lax.ppermute(wide, SECTION + COPY, turn)  6.44 us
    ppermute x1, starting transfers between devices, gather_rows(): rows = jnp.concatenate([own, lax.ppermute(own, 'core', swap)], axis=0)  5.33 us
  transfers between devices with their start and end apart: 7, of which 6 were waited for; matrix products, arithmetic and copies ran while one was open for 5% of the time, Pallas kernels for 0%

profile of v1, /device:TPU:1, one launch (start us, length us, event | category | flops | bytes accessed | tf_op | source)
XLA Modules:
  0.0 142.3 jit_solution(16582973310904266087)
XLA Ops:
  0.0 0.0 copy-start
  0.0 0.0 copy-start.3
  0.0 0.0 copy-start.5
  0.0 1.1 broadcast_in_dim.8
  1.1 1.0 broadcast_in_dim.9
  2.0 13.2 %all-to-all-start = ((bf16[16,24,1024]{2,1,0:T(8,128)(2,1)}), bf16[16,24,1024]{2,1,0:T(8,128)(2,1)S(1)}, u32[]{:S(2)}, u32[]{:S(2)}) async-start(bf16[16,24,1024]{2,1,0:T(8,128)(2,1)} %broadcast_in_dim.9), calls=%async_computation | async-start | bytes 1572864 | tf_op jit(solution)/shard_map/all_to_all | solution.py:17
  15.2 1.7 %copy.27 = bf16[16,8,8,128]{3,2,1,0:T(8,128)(2,1)} copy(bf16[16,8,8,128]{3,1,2,0:T(8,128)(2,1)} %bitcast.94) | data formatting | bytes 524288
  16.9 0.0 copy-done.3
  19.0 0.0 copy-done.5
  19.0 0.5 bitcast_convert_fusion
  19.5 18.6 %all-to-all-done = bf16[16,24,1024]{2,1,0:T(8,128)(2,1)S(1)} async-done(((bf16[16,24,1024]{2,1,0:T(8,128)(2,1)}), bf16[16,24,1024]{2,1,0:T(8,128)(2,1)S(1)}, u32[]{:S(2)}, u32[]{:S(2)}) %all-to-all-start) | async-done | bytes 786464 | tf_op jit(solution)/shard_map/all_to_all | solution.py:17
  38.1 0.8 fusion.87
  38.9 0.9 slice.19
  39.9 3.0 %collective-permute-start = (bf16[24,8192]{1,0:T(8,128)(2,1)}, bf16[24,8192]{1,0:T(8,128)(2,1)S(1)}, u32[]{:S(2)}, u32[]{:S(2)}) collective-permute-start(bf16[24,8192]{1,0:T(8,128)(2,1)} %slice.19), channel_id=1, source_target_pairs={{0,8},{8,16},{16,24},{24,32},{32,40},{40,48},{48,56},{56,0},{1,9},... | collective-permute-start | bytes 1179656 | tf_op jit(solution)/shard_map/ppermute | solution.py:21
  42.8 2.0 %slice.21 = bf16[24,8192]{1,0:T(8,128)(2,1)} reshape(bf16[8,24,1024]{2,1,0:T(8,128)(2,1)} %get-tuple-element.5) | data formatting | bytes 786432 | tf_op jit(solution)/shard_map/slice | solution.py:22
  44.8 3.5 %collective-permute-start.1 = (bf16[24,8192]{1,0:T(8,128)(2,1)}, bf16[24,8192]{1,0:T(8,128)(2,1)}, u32[]{:S(2)}, u32[]{:S(2)}) collective-permute-start(bf16[24,8192]{1,0:T(8,128)(2,1)} %slice.21), channel_id=1, source_target_pairs={{0,56},{8,0},{16,8},{24,16},{32,24},{40,32},{48,40},{56,48},{1,57}... | collective-permute-start | bytes 1179656 | tf_op jit(solution)/shard_map/ppermute | solution.py:22
  48.3 1.2 reshape.163
  49.5 1.2 constant_dynamic-update-slice_fusion.3
  50.7 0.0 collective-permute-done
  50.7 4.5 %collective-permute-done.1 = bf16[24,8192]{1,0:T(8,128)(2,1)} collective-permute-done((bf16[24,8192]{1,0:T(8,128)(2,1)}, bf16[24,8192]{1,0:T(8,128)(2,1)}, u32[]{:S(2)}, u32[]{:S(2)}) %collective-permute-start.1) | collective-permute-done | bytes 393248 | tf_op jit(solution)/shard_map/ppermute | solution.py:22
  55.2 1.4 pad_maximum_fusion
  56.6 0.0 copy-start.2
  56.6 5.3 %collective-permute-start.2 = (bf16[96,8192]{1,0:T(8,128)(2,1)S(1)}, bf16[96,8192]{1,0:T(8,128)(2,1)S(1)}, u32[]{:S(2)}, u32[]{:S(2)}) collective-permute-start(bf16[96,8192]{1,0:T(8,128)(2,1)S(1)} %pad_maximum_fusion), channel_id=1, source_target_pairs={{0,64},{64,0},{1,65},{65,1},{2,66},{66,2},{3,67},{67,3},{4,68},{68... | collective-permute-start | bytes 4718600 | tf_op jit(solution)/shard_map/ppermute | solution.py:25
  62.0 1.0 constant_dynamic-update-slice_fusion.1
  63.0 2.0 %collective-permute-done.2 = bf16[96,8192]{1,0:T(8,128)(2,1)S(1)} collective-permute-done((bf16[96,8192]{1,0:T(8,128)(2,1)S(1)}, bf16[96,8192]{1,0:T(8,128)(2,1)S(1)}, u32[]{:S(2)}, u32[]{:S(2)}) %collective-permute-start.2) | collective-permute-done | bytes 1572896 | tf_op jit(solution)/shard_map/ppermute | solution.py:25
  65.0 0.1 constant_dynamic-update-slice_fusion
  65.1 0.0 copy-done.2
  65.1 0.0 copy-start.1
  65.1 1.1 multiply_reduce_fusion.2
  66.2 0.5 copy-done.1
  66.8 0.0 copy-done
  66.8 0.0 copy-start.4
  66.8 0.0 copy-start.6
  66.8 3.1 %convolution_bitcast_fusion = f32[8,128,192]{1,2,0:T(8,128)S(1)} fusion(bf16[192,8192]{1,0:T(8,128)(2,1)} %copy-done.1, bf16[1,8192,128]{2,1,0:T(8,128)(2,1)S(1)} %copy-done, bf16[128,8,128]{2,1,0:T(8,128)(2,1)S(1)} %bitcast.92, bf16[128]{0:T(256)(128)(2,1)S(1)} %compare_convert_fusion), kind=kOutput, calls=%fused_computation.17 | convolution fusion | flops 453533696 | bytes 6291712 | tf_op jit(solution)/shard_map/tgd,vd->gtv/dot_general | solution.py:61
  69.9 0.0 copy-done.4
  69.9 0.0 copy-done.6
  69.9 1.3 fusion.88
  71.2 0.0 copy-start.8
  71.2 1.2 fusion.20
  72.4 0.0 copy-done.8
  72.4 0.0 copy-start.7
  72.4 1.9 %multiply_reduce_fusion.1 = (f32[192]{0:T(256)S(1)}, f32[192,128]{1,0:T(8,128)S(1)}) fusion(f32[192,128]{1,0:T(8,128)S(1)} %get-tuple-element.8, f32[128]{0:T(128)} %bitcast_convert_fusion, bf16[128,8,128]{2,1,0:T(8,128)(2,1)S(1)} %bitcast.98, f32[8,128,192]{1,2,0:T(8,128)S(1)} %convolution_bitcast_fusion, f32[8,128,192]{1,2,0:T(8,128)} %get-tuple-element.10, ...), kind=kOutput, calls=%fused_computation.51 | convolution fusion | flops 51782656 | bytes 2036992 | tf_op jit(solution)/shard_map/gtv,tgd->vd/dot_general | solution.py:63
  74.3 0.1 fusion.39
  74.4 0.0 copy-done.7
  74.4 0.8 convolution_convert_fusion
  75.3 9.8 %all-to-all-start.1 = ((bf16[8,32,256]{2,1,0:T(8,128)(2,1)}), bf16[8,32,256]{2,1,0:T(8,128)(2,1)S(1)}, u32[]{:S(2)}, u32[]{:S(2)}) async-start(bf16[8,32,256]{2,1,0:T(8,128)(2,1)} %bitcast.12), calls=%async_computation.1 | async-start | bytes 262144 | tf_op jit(solution)/shard_map/all_to_all | solution.py:71
  85.0 9.5 %all-to-all-done.1 = bf16[8,32,256]{2,1,0:T(8,128)(2,1)S(1)} async-done(((bf16[8,32,256]{2,1,0:T(8,128)(2,1)}), bf16[8,32,256]{2,1,0:T(8,128)(2,1)S(1)}, u32[]{:S(2)}, u32[]{:S(2)}) %all-to-all-start.1) | async-done | bytes 131104 | tf_op jit(solution)/shard_map/all_to_all | solution.py:71
  94.5 2.4 %fusion.6 = f32[32,8192]{1,0:T(8,128)S(1)} fusion(bf16[1,8192,128]{2,1,0:T(8,128)(2,1)} %param.10, bf16[32,256]{1,0:T(8,128)(2,1)S(1)} %reduce_sum.68), kind=kOutput, calls=%fused_computation.7 | convolution fusion | flops 67108864 | bytes 3153920 | tf_op jit(solution)/shard_map/bk,dk->bd/dot_general | solution.py:73
  96.9 0.8 fusion.2
  97.7 0.4 reshape.165
  98.1 0.3 copy.24
  98.5 3.7 %collective-permute-start.3 = (bf16[32,32,128]{2,1,0:T(8,128)(2,1)S(1)}, bf16[32,32,128]{2,1,0:T(8,128)(2,1)S(1)}, u32[]{:S(2)}, u32[]{:S(2)}) collective-permute-start(bf16[32,32,128]{2,1,0:T(8,128)(2,1)S(1)} %dynamic-slice_bitcast_fusion), channel_id=1, source_target_pairs={{0,64},{64,0},{1,65},{65,1},{2,66},{66,2},{3,67},{67,3},{4,68},{68... | collective-permute-start | bytes 786440 | tf_op jit(solution)/shard_map/ppermute | solution.py:80
  102.2 1.1 collective-permute-done.3
  103.4 0.1 fusion.31
  103.5 17.7 %all_to_all.20 = bf16[32,32,128]{2,1,0:T(8,128)(2,1)S(1)} all-to-all(bf16[32,32,128]{2,1,0:T(8,128)(2,1)S(1)} %fusion.31), channel_id=1, replica_groups=mesh['zl'=4,'core'=2,'yh'=4,'yl'=2,'x'=4,'zh'=2] {'zl','yh','yl'}, dimensions={0} | all-to-all | bytes 524288 | tf_op jit(solution)/shard_map/all_to_all | solution.py:82
  121.1 0.1 reduce_sum.69
  121.2 11.0 %all_to_all.21 = bf16[8,32,128]{2,1,0:T(8,128)(2,1)S(1)} all-to-all(bf16[8,32,128]{2,1,0:T(8,128)(2,1)S(1)} %broadcast_in_dim.11), channel_id=1, replica_groups=mesh['zl'=4,'core'=2,'yh'=4,'yl'=2,'x'=4,'zh'=2] {'zl','core'}, dimensions={0} | all-to-all | bytes 131072 | tf_op jit(solution)/shard_map/all_to_all | solution.py:84
  132.2 3.0 %collective-permute-start.4 = (bf16[8,32,128]{2,1,0:T(8,128)(2,1)S(1)}, bf16[8,32,128]{2,1,0:T(8,128)(2,1)S(1)}, u32[]{:S(2)}, u32[]{:S(2)}) collective-permute-start(bf16[8,32,128]{2,1,0:T(8,128)(2,1)S(1)} %all_to_all.21), channel_id=1, source_target_pairs={{0,0},{1,64},{2,128},{3,192},{4,256},{5,320},{6,384},{7,448},{64,1... | collective-permute-start | bytes 196616 | tf_op jit(solution)/shard_map/ppermute | solution.py:86
  135.2 6.4 %collective-permute-done.4 = bf16[8,32,128]{2,1,0:T(8,128)(2,1)S(1)} collective-permute-done((bf16[8,32,128]{2,1,0:T(8,128)(2,1)S(1)}, bf16[8,32,128]{2,1,0:T(8,128)(2,1)S(1)}, u32[]{:S(2)}, u32[]{:S(2)}) %collective-permute-start.4) | collective-permute-done | bytes 65568 | tf_op jit(solution)/shard_map/ppermute | solution.py:86
  141.7 0.7 copy_bitcast_fusion
  (9 shorter events, 0.2 us)
Async XLA Ops:
  0.0 66.8 %copy-start = (bf16[1,8192,128]{2,1,0:T(8,128)(2,1)S(1)}, bf16[1,8192,128]{2,1,0:T(8,128)(2,1)}, u32[]{:S(2)}) copy-start(bf16[1,8192,128]{2,1,0:T(8,128)(2,1)} %param.11) | copy-start | bytes 6291460
  0.0 16.9 %copy-start.3 = (bf16[1,1,128,1024]{3,2,1,0:T(8,128)(2,1)S(1)}, bf16[1,1,128,1024]{3,2,1,0:T(8,128)(2,1)}, u32[]{:S(2)}) copy-start(bf16[1,1,128,1024]{3,2,1,0:T(8,128)(2,1)} %param.14) | copy-start | bytes 786436
  0.0 19.0 %copy-start.5 = (bf16[1,128]{1,0:T(2,128)(2,1)S(1)}, bf16[1,128]{1,0:T(2,128)(2,1)}, u32[]{:S(2)}) copy-start(bf16[1,128]{1,0:T(2,128)(2,1)} %param.12) | copy-start | bytes 772
  2.0 36.1 %all-to-all-start = ((bf16[16,24,1024]{2,1,0:T(8,128)(2,1)}), bf16[16,24,1024]{2,1,0:T(8,128)(2,1)S(1)}, u32[]{:S(2)}, u32[]{:S(2)}) async-start(bf16[16,24,1024]{2,1,0:T(8,128)(2,1)} %broadcast_in_dim.9), calls=%async_computation | async-start | bytes 1572864 | tf_op jit(solution)/shard_map/all_to_all | solution.py:17
  39.9 10.9 %collective-permute-start = (bf16[24,8192]{1,0:T(8,128)(2,1)}, bf16[24,8192]{1,0:T(8,128)(2,1)S(1)}, u32[]{:S(2)}, u32[]{:S(2)}) collective-permute-start(bf16[24,8192]{1,0:T(8,128)(2,1)} %slice.19), channel_id=1, source_target_pairs={{0,8},{8,16},{16,24},{24,32},{32,40},{40,48},{48,56},{56,0},{1,9},... | collective-permute-start | bytes 1179656 | tf_op jit(solution)/shard_map/ppermute | solution.py:21
  44.8 10.4 %collective-permute-start.1 = (bf16[24,8192]{1,0:T(8,128)(2,1)}, bf16[24,8192]{1,0:T(8,128)(2,1)}, u32[]{:S(2)}, u32[]{:S(2)}) collective-permute-start(bf16[24,8192]{1,0:T(8,128)(2,1)} %slice.21), channel_id=1, source_target_pairs={{0,56},{8,0},{16,8},{24,16},{32,24},{40,32},{48,40},{56,48},{1,57}... | collective-permute-start | bytes 1179656 | tf_op jit(solution)/shard_map/ppermute | solution.py:22
  56.6 8.5 %copy-start.2 = (bf16[1,8192,128]{2,1,0:T(8,128)(2,1)S(1)}, bf16[1,8192,128]{2,1,0:T(8,128)(2,1)}, u32[]{:S(2)}) copy-start(bf16[1,8192,128]{2,1,0:T(8,128)(2,1)} %param.10) | copy-start | bytes 6291460
  56.6 8.4 %collective-permute-start.2 = (bf16[96,8192]{1,0:T(8,128)(2,1)S(1)}, bf16[96,8192]{1,0:T(8,128)(2,1)S(1)}, u32[]{:S(2)}, u32[]{:S(2)}) collective-permute-start(bf16[96,8192]{1,0:T(8,128)(2,1)S(1)} %pad_maximum_fusion), channel_id=1, source_target_pairs={{0,64},{64,0},{1,65},{65,1},{2,66},{66,2},{3,67},{67,3},{4,68},{68... | collective-permute-start | bytes 4718600 | tf_op jit(solution)/shard_map/ppermute | solution.py:25
  65.1 1.7 %copy-start.1 = (bf16[192,8192]{1,0:T(8,128)(2,1)}, bf16[192,8192]{1,0:T(8,128)(2,1)S(1)}, u32[]{:S(2)}) copy-start(bf16[192,8192]{1,0:T(8,128)(2,1)S(1)} %constant_dynamic-update-slice_fusion) | copy-start | bytes 9437188
  66.8 3.1 %copy-start.4 = (bf16[16,8,8,128]{3,2,1,0:T(8,128)(2,1)S(1)}, bf16[16,8,8,128]{3,2,1,0:T(8,128)(2,1)}, u32[]{:S(2)}) copy-start(bf16[16,8,8,128]{3,2,1,0:T(8,128)(2,1)} %copy.27) | copy-start | bytes 786436
  66.8 3.1 %copy-start.6 = (f32[128]{0:T(128)S(1)}, f32[128]{0:T(128)}, u32[]{:S(2)}) copy-start(f32[128]{0:T(128)} %bitcast_convert_fusion) | copy-start | bytes 1540
  71.2 1.2 copy-start.8
  72.4 2.0 %copy-start.7 = (bf16[192,128]{1,0:T(8,128)(2,1)S(1)}, bf16[192,128]{1,0:T(8,128)(2,1)}, u32[]{:S(2)}) copy-start(bf16[192,128]{1,0:T(8,128)(2,1)} %fusion.20) | copy-start | bytes 147460
  75.3 19.2 %all-to-all-start.1 = ((bf16[8,32,256]{2,1,0:T(8,128)(2,1)}), bf16[8,32,256]{2,1,0:T(8,128)(2,1)S(1)}, u32[]{:S(2)}, u32[]{:S(2)}) async-start(bf16[8,32,256]{2,1,0:T(8,128)(2,1)} %bitcast.12), calls=%async_computation.1 | async-start | bytes 262144 | tf_op jit(solution)/shard_map/all_to_all | solution.py:71
  98.5 4.9 %collective-permute-start.3 = (bf16[32,32,128]{2,1,0:T(8,128)(2,1)S(1)}, bf16[32,32,128]{2,1,0:T(8,128)(2,1)S(1)}, u32[]{:S(2)}, u32[]{:S(2)}) collective-permute-start(bf16[32,32,128]{2,1,0:T(8,128)(2,1)S(1)} %dynamic-slice_bitcast_fusion), channel_id=1, source_target_pairs={{0,64},{64,0},{1,65},{65,1},{2,66},{66,2},{3,67},{67,3},{4,68},{68... | collective-permute-start | bytes 786440 | tf_op jit(solution)/shard_map/ppermute | solution.py:80
  132.2 9.5 %collective-permute-start.4 = (bf16[8,32,128]{2,1,0:T(8,128)(2,1)S(1)}, bf16[8,32,128]{2,1,0:T(8,128)(2,1)S(1)}, u32[]{:S(2)}, u32[]{:S(2)}) collective-permute-start(bf16[8,32,128]{2,1,0:T(8,128)(2,1)S(1)} %all_to_all.21), channel_id=1, source_target_pairs={{0,0},{1,64},{2,128},{3,192},{4,256},{5,320},{6,384},{7,448},{64,1... | collective-permute-start | bytes 196616 | tf_op jit(solution)/shard_map/ppermute | solution.py:86

commit v2 on v1

v2 whole, which is shorter than its diff:
```python
import functools

import jax
import jax.numpy as jnp
from jax import lax
from jax.experimental import pallas as pl
from jax.experimental.pallas import tpu as pltpu
from jax.sharding import Mesh, PartitionSpec as P

GW = 24
BW = 32
EPS = 1e-05
SECTION = ("zl", "core")
TENSOR = ("yh", "yl")
COPY = ("x", "zh")
STEP = 2048
SWAP = [(0, 1), (1, 0)]
NT = (((1,), (1,)), ((), ()))
F32 = jnp.float32
BF16 = jnp.bfloat16


def factors_kernel(
    length, target, same, other, far_same, far_other, w_key, w_value, gain, query, grad, out, late, rows, sems
):
    pieces = (same, other, far_same, far_other)

    def load(step, i):
        part = pl.ds(step * STEP, STEP)
        return pltpu.make_async_copy(pieces[i].at[:, part], rows.at[pl.ds(48 * i, 48), part], sems.at[step, i])

    def bring(step):
        part = pl.ds(step * STEP, STEP)
        return pltpu.make_async_copy(w_value.at[part, :], late.at[part, :], sems.at[step, 4])

    steps = 8192 // STEP
    for step in range(steps):
        bring(step).start()
        for i in range(4):
            load(step, i).start()
    both = jnp.zeros((192, 256), F32)
    for step in range(steps):
        part = pl.ds(step * STEP, STEP)
        for i in range(4):
            load(step, i).wait()
        bring(step).wait()
        mats = jnp.concatenate([w_key[part, :], late[part, :]], axis=1)
        both += jnp.dot(rows[:, part], mats, preferred_element_type=F32)
    kraw = both[:, :128]
    values = both[:, 128:].astype(BF16)
    scale_row = lax.rsqrt(jnp.mean(kraw * kraw, axis=1, keepdims=True) + EPS)
    gains = gain[...].astype(F32)
    keys = (kraw * scale_row * gains).astype(BF16)
    scale = 128 ** (-0.5)
    text = lax.broadcasted_iota(jnp.int32, (128, 128), 0)
    live = text < length[0]
    dval = jnp.zeros((192, 128), F32)
    dkey = jnp.zeros((192, 128), F32)
    for g in range(8):
        lanes = pl.ds(g * 128, 128)
        q = query[:, lanes]
        dout = jnp.where(live, grad[:, lanes].astype(F32), 0.0).astype(BF16)
        scores = lax.dot_general(keys, q, NT, preferred_element_type=F32) * scale
        dprob = lax.dot_general(values, dout, NT, preferred_element_type=F32)
        grown = jnp.exp(scores - jnp.max(scores, axis=0, keepdims=True))
        probs = grown / jnp.sum(grown, axis=0, keepdims=True)
        inner = jnp.sum(probs * dprob, axis=0, keepdims=True)
        dscore = probs * (dprob - inner) * scale
        dval += jnp.dot(probs.astype(BF16), dout, preferred_element_type=F32)
        dkey += jnp.dot(dscore.astype(BF16), q, preferred_element_type=F32)
    dn = dkey * gains
    dot_row = jnp.sum(dn * kraw, axis=1, keepdims=True) * (1.0 / 128)
    dkraw = dn * scale_row - kraw * (scale_row * scale_row * scale_row * dot_row)
    fac = jnp.concatenate([dkraw.astype(BF16), dval.astype(BF16)], axis=1)
    patch = lax.broadcasted_iota(jnp.int32, (256, 192), 0)
    onehot = (patch == target[...]).astype(F32).astype(BF16)
    out[...] = jnp.dot(onehot, fac, preferred_element_type=F32).astype(BF16)


def product_kernel(mine, parts, w_key, w_value, keep, give):
    total = jnp.zeros((BW, 256), F32)
    for c in range(8):
        total += parts[c].astype(F32)
    total = total.astype(BF16)
    first = mine[0] == 0
    for y in range(8):
        part = pl.ds(y * 1024, 1024)
        mats = jnp.concatenate([w_key[part, :], w_value[part, :]], axis=1)
        wide = lax.dot_general(total, mats, NT, preferred_element_type=F32)
        for zl in range(4):
            left = wide[:, zl * 256 : zl * 256 + 128]
            right = wide[:, zl * 256 + 128 : zl * 256 + 256]
            keep[zl * 8 + y] = jnp.where(first, left, right).astype(BF16)
            give[zl * 8 + y] = jnp.where(first, right, left).astype(BF16)


def in_hbm(array):
    return pltpu.with_memory_space_constraint(array, pltpu.HBM)


def call(kernel, scalars, arrays, out_shape, limit, flops, kept=(), scratch=()):
    smem = pl.BlockSpec(memory_space=pltpu.SMEM)
    vmem = pl.BlockSpec(memory_space=pltpu.VMEM)
    whole = pl.BlockSpec(memory_space=pltpu.HBM)
    return pl.pallas_call(
        kernel,
        in_specs=[smem] * len(scalars) + [whole if i in kept else vmem for i in range(len(arrays))],
        out_specs=jax.tree.map(lambda _: vmem, out_shape),
        out_shape=out_shape,
        scratch_shapes=list(scratch),
        compiler_params=pltpu.CompilerParams(vmem_limit_bytes=limit),
        cost_estimate=pl.CostEstimate(flops=flops, bytes_accessed=8 << 20, transcendentals=0),
    )(*scalars, *arrays)


def on_device(visual, w_key, w_value, key_gain, queries, grad_out, offsets, flips, lengths):
    core = lax.axis_index("core")
    spread = jnp.broadcast_to(visual[0].reshape(1, 24, 1024), (16, 24, 1024))
    same = lax.all_to_all(spread, ("zl", "yh"), 0, 0).reshape(48, 8192)
    walk = [(k * 8 + (y + 1 - 2 * k) % 8, k * 8 + y) for k in range(2) for y in range(8)]
    other = lax.ppermute(same, ("core",) + TENSOR, walk)
    far_same = lax.ppermute(same, "core", SWAP)
    far_other = lax.ppermute(other, "core", SWAP)
    rows = [same, other, far_same, far_other]
    r = jnp.arange(192, dtype=jnp.int32)
    line = ((r // 12) % 4) * 2 + (core + r // 96) % 2
    parity = (lax.axis_index("yl") + (r // 48) % 2) % 2
    column = (((r // 3) % 4) * 2 + parity) * 3 + r % 3
    target = line * BW + offsets[0] + jnp.where(flips[0] == 1, GW - 1 - column, column)
    key_mat, value_mat = w_key[0], w_value[0]
    placed, value_mat = call(
        factors_kernel,
        [lengths],
        [target[None], *map(in_hbm, rows), key_mat, in_hbm(value_mat), key_gain, queries[0, 0], grad_out[0, 0]],
        (jax.ShapeDtypeStruct((256, 256), BF16), jax.ShapeDtypeStruct((8192, 128), BF16)),
        12 << 20,
        1 << 30,
        kept=(1, 2, 3, 4, 6),
        scratch=[pltpu.VMEM((192, 8192), BF16), pltpu.SemaphoreType.DMA((8192 // STEP, 5))],
    )
    parts = lax.all_to_all(placed.reshape(8, BW, 256), COPY, 0, 0)
    block = jax.ShapeDtypeStruct((32, BW, 128), BF16)
    keep, give = call(
        product_kernel, [core.astype(jnp.int32)[None]], [parts, key_mat, value_mat], (block, block), 8 << 20, 1 << 27
    )
    got = lax.ppermute(give, "core", SWAP)
    pair = (keep.astype(F32) + got.astype(F32)).astype(BF16)
    pieces = lax.all_to_all(pair, ("zl",) + TENSOR, 0, 0)
    total = jnp.sum(pieces.astype(F32), axis=0).astype(BF16)
    wide = lax.all_to_all(jnp.broadcast_to(total[None], (8, BW, 128)), SECTION, 0, 0)
    out = lax.ppermute(wide, SECTION + COPY, turn())
    return out.transpose(1, 0, 2).reshape(BW, 1024).astype(F32)


def turn():
    pairs = []
    for row in range(8):
        x, zh = row // 2, row % 2
        senders = sorted(range(8), key=lambda s: abs(s // 2 - x))
        for side in range(2):
            along = lambda s: abs(s // 2 - x) if side == 0 else 4 - abs(s // 2 - x)
            order = sorted(senders[4 * side : 4 * side + 4], key=along)
            close = sorted(range(4), key=lambda other: -min((other - x) % 4, (x - other) % 4))
            for s, to_x in zip(order, close):
                pairs.append((s * 8 + row, row * 8 + to_x * 2 + (zh ^ side)))
    return pairs


def solution(mesh):
    fine = Mesh(mesh.devices.reshape(4, 2, 4, 2, 4, 2), ("zl", "core", "yh", "yl", "x", "zh"))
    placed = (
        P(COPY, SECTION + TENSOR, None),
        P(SECTION, None, TENSOR),
        P(SECTION, None, TENSOR),
        P(SECTION, TENSOR),
        P(SECTION, COPY, None, TENSOR),
        P(SECTION, COPY, None, TENSOR),
        P(COPY),
        P(COPY),
        P(COPY),
    )
    return jax.shard_map(
        on_device, mesh=fine, in_specs=placed, out_specs=P(SECTION, TENSOR), check_vma=False
    )
```

time: 143 us -> 126 us (0.88)
  blocking collectives: 28.7 us -> 82.2 us
  waiting for transfers between devices: 42.1 us -> 14 us
  starting transfers between devices: 41.5 us -> 16 us
  matrix products: 12.7 us -> 0 us
  local copies, waits for them, and re-layouts: 12.3 us -> 2.63 us
  Pallas kernels: 0 us -> 7.18 us
  other arithmetic: 2.87 us -> 0.83 us
    all_to_all x1 -> x3, blocking collectives: 17.7 us -> 71.2 us  [the longest x1 37 us: on_device(): same = lax.all_to_all(spread, ('zl', 'yh'), 0, 0).reshape(48, 8192)]
    all_to_all x2 -> x0, waiting for transfers between devices: 28.1 us -> none  [the longest x1 18.6 us: gather_rows(): same = lax.all_to_all(spread, ('zl', 'yh'), 0, 0)]
    all_to_all x2 -> x0, starting transfers between devices: 22.9 us -> none  [the longest x1 13.2 us: gather_rows(): same = lax.all_to_all(spread, ('zl', 'yh'), 0, 0)]
    dot_general x7 -> x0, matrix products: 11.4 us -> none  [the longest x1 3.09 us: on_device(): jnp.einsum('tgd,vd->gtv', dout, values, preferred_element_type=jnp.float32)]
    pallas_call x0 -> x2, Pallas kernels: none -> 7.18 us  [call(): pl.pallas_call(kernel, in_specs=[smem] * len(scalars) + [whole if i in ke...]
    unnamed x23 -> x10, local copies, waits for them, and re-layouts: 4.55 us -> 0.02 us
    slice x3 -> x0, local copies, waits for them, and re-layouts: 3.67 us -> none  [the longest x2 2.74 us: gather_rows(): high = lax.ppermute(same[24:], TENSOR, down)]
    ppermute x5, starting transfers between devices: 18.6 us -> 16 us  [the longest x1 3.76 us: on_device(): far_other = lax.ppermute(other, 'core', SWAP)]
  transfers between devices with their start and end apart: 7 -> 5, of which waited for: 6 -> 4; matrix products, arithmetic and copies ran while one was open for 5% -> 0% of each run, Pallas kernels for 0% -> 0%
where the time goes in v2:
time: 126 us; the launch traced here: 125 us
  blocking collectives  82.2 us (65%)
  starting transfers between devices  16 us (13%)
  waiting for transfers between devices  14 us (11%)
  Pallas kernels  7.18 us (6%)
  local copies, waits for them, and re-layouts  2.63 us (2%)
  between operations  2.07 us (2%)
    all_to_all x1, blocking collectives, on_device(): same = lax.all_to_all(spread, ('zl', 'yh'), 0, 0).reshape(48, 8192)  37 us
    all_to_all x1, blocking collectives, on_device(): parts = lax.all_to_all(placed.reshape(8, BW, 256), COPY, 0, 0)  19 us
    all_to_all x1, blocking collectives, on_device(): pieces = lax.all_to_all(pair, ('zl',) + TENSOR, 0, 0)  15.2 us
    all_to_all x1, blocking collectives, on_device(): lax.all_to_all(jnp.broadcast_to(total[None], (8, BW, 128)), SECTION, 0, 0)  11 us
    ppermute x1, waiting for transfers between devices, on_device(): other = lax.ppermute(same, ('core',) + TENSOR, walk)  8.28 us
    pallas_call x2, Pallas kernels, call(): pl.pallas_call(kernel, in_specs=[smem] * len(scalars) + [whole if i in ke...  7.18 us
    ppermute x1, waiting for transfers between devices, on_device(): out = lax.ppermute(wide, SECTION + COPY, turn())  4.39 us
    ppermute x1, starting transfers between devices, on_device(): far_other = lax.ppermute(other, 'core', SWAP)  3.76 us
  transfers between devices with their start and end apart: 5, of which 4 were waited for; matrix products, arithmetic and copies ran while one was open for 0% of the time, Pallas kernels for 0%

profile of v2, /device:TPU:1, one launch (start us, length us, event | category | flops | bytes accessed | tf_op | source)
XLA Modules:
  0.0 124.9 jit_solution(3396489172720271657)
XLA Ops:
  0.0 0.0 copy-start.2
  0.0 0.0 copy-start.1
  0.0 0.0 copy-start.3
  0.0 0.0 copy-start
  0.0 1.1 broadcast_in_dim.18
  1.1 0.1 broadcast_in_dim.19
  1.2 37.0 %all_to_all.20 = bf16[16,24,1024]{2,1,0:T(8,128)(2,1)} all-to-all(bf16[16,24,1024]{2,1,0:T(8,128)(2,1)S(1)} %broadcast_in_dim.19), channel_id=1, replica_groups=mesh['zl'=4,'core'=2,'yh'=4,'yl'=2,'x'=4,'zh'=2] {'zl','yh'}, dimensions={0} | all-to-all | bytes 1572864 | tf_op jit(solution)/shard_map/all_to_all | solution.py:119
  38.1 1.4 %reshape.335.same = bf16[48,8192]{1,0:T(8,128)(2,1)S(1)} reshape(bf16[16,24,1024]{2,1,0:T(8,128)(2,1)} %all_to_all.20) | data formatting | bytes 1572864 | tf_op jit(solution)/shard_map/reshape | solution.py:119
  39.6 0.0 copy-start.4
  39.6 2.2 %collective-permute-start = (bf16[48,8192]{1,0:T(8,128)(2,1)S(1)}, bf16[48,8192]{1,0:T(8,128)(2,1)}, u32[]{:S(2)}, u32[]{:S(2)}) collective-permute-start(bf16[48,8192]{1,0:T(8,128)(2,1)S(1)} %reshape.335.same), channel_id=1, source_target_pairs={{8,0},{16,8},{24,16},{32,24},{40,32},{48,40},{56,48},{0,56},{120,6... | collective-permute-start | bytes 2359304 | tf_op jit(solution)/shard_map/ppermute | solution.py:121
  41.8 3.5 %collective-permute-start.1 = (bf16[48,8192]{1,0:T(8,128)(2,1)S(1)}, bf16[48,8192]{1,0:T(8,128)(2,1)}, u32[]{:S(2)}, u32[]{:S(2)}) collective-permute-start(bf16[48,8192]{1,0:T(8,128)(2,1)S(1)} %reshape.335.same), channel_id=1, source_target_pairs={{0,64},{64,0},{1,65},{65,1},{2,66},{66,2},{3,67},{67,3},{4,68},{68... | collective-permute-start | bytes 2359304 | tf_op jit(solution)/shard_map/ppermute | solution.py:122
  45.4 8.3 %collective-permute-done.other = bf16[48,8192]{1,0:T(8,128)(2,1)} collective-permute-done((bf16[48,8192]{1,0:T(8,128)(2,1)S(1)}, bf16[48,8192]{1,0:T(8,128)(2,1)}, u32[]{:S(2)}, u32[]{:S(2)}) %collective-permute-start) | collective-permute-done | bytes 786464 | tf_op jit(solution)/shard_map/ppermute | solution.py:121
  53.6 3.8 %collective-permute-start.2 = (bf16[48,8192]{1,0:T(8,128)(2,1)}, bf16[48,8192]{1,0:T(8,128)(2,1)}, u32[]{:S(2)}, u32[]{:S(2)}) collective-permute-start(bf16[48,8192]{1,0:T(8,128)(2,1)} %collective-permute-done.other), channel_id=1, source_target_pairs={{0,64},{64,0},{1,65},{65,1},{2,66},{66,2},{3,67},{67,3},{4,68},{68... | collective-permute-start | bytes 2359304 | tf_op jit(solution)/shard_map/ppermute | solution.py:123
  59.4 0.0 collective-permute-done.1.far_same
  59.4 0.2 collective-permute-done.2.far_other
  59.6 0.0 copy-done.4
  59.6 0.0 copy-done.2
  59.6 0.0 copy-done.1
  59.6 0.0 copy-done.3
  59.7 0.0 copy-done
  59.7 5.8 %shard_map.91 = (bf16[256,256]{1,0:T(8,128)(2,1)S(1)}, bf16[8192,128]{1,0:T(8,128)(2,1)S(1)}) custom-call(s32[1]{0:T(128)S(6)} %copy.15.length, s32[1,192]{1,0:T(1,128)S(1)} %fusion.3.target, bf16[48,8192]{1,0:T(8,128)(2,1)} %copy-done.4, bf16[48,8192]{1,0:T(8,128)(2,1)} %collective-permute-done.other, bf16[48,8192]{1,0:T(8,128)(2,1)} %collective-permute-done.1.far_same, ...), custom_call_target="tpu_custom_call" | custom-call | flops 1073741824 | bytes 8388608 | tf_op jit(solution)/shard_map/pallas_call | solution.py:105
  65.5 19.0 %all_to_all.21.parts = bf16[8,32,256]{2,1,0:T(8,128)(2,1)S(1)} all-to-all(bf16[8,32,256]{2,1,0:T(8,128)(2,1)S(1)} %bitcast.19), channel_id=1, replica_groups=mesh['zl'=4,'core'=2,'yh'=4,'yl'=2,'x'=4,'zh'=2] {'x','zh'}, dimensions={0} | all-to-all | bytes 262144 | tf_op jit(solution)/shard_map/all_to_all | solution.py:141
  84.5 1.3 %shard_map.92 = (bf16[32,32,128]{2,1,0:T(8,128)(2,1)S(1)}, bf16[32,32,128]{2,1,0:T(8,128)(2,1)S(1)}) custom-call(s32[1]{0:T(128)} %bitcast.mine, bf16[8,32,256]{2,1,0:T(8,128)(2,1)S(1)} %all_to_all.21.parts, bf16[8192,128]{1,0:T(8,128)(2,1)S(1)} %bitcast.16, bf16[8192,128]{1,0:T(8,128)(2,1)S(1)} %get-tuple-element.10.w_value), custom_call_target="tpu_custom_call" | custom-call | flops 134217728 | bytes 8388608 | tf_op jit(solution)/shard_map/pallas_call | solution.py:105
  85.9 3.7 %collective-permute-start.3 = (bf16[32,32,128]{2,1,0:T(8,128)(2,1)S(1)}, bf16[32,32,128]{2,1,0:T(8,128)(2,1)S(1)}, u32[]{:S(2)}, u32[]{:S(2)}) collective-permute-start(bf16[32,32,128]{2,1,0:T(8,128)(2,1)S(1)} %get-tuple-element.12), channel_id=1, source_target_pairs={{0,64},{64,0},{1,65},{65,1},{2,66},{66,2},{3,67},{67,3},{4,68},{68... | collective-permute-start | bytes 786440 | tf_op jit(solution)/shard_map/ppermute | solution.py:146
  89.6 1.1 collective-permute-done.3
  90.8 0.1 add_convert_fusion
  90.8 15.2 %all_to_all.22 = bf16[32,32,128]{2,1,0:T(8,128)(2,1)S(1)} all-to-all(bf16[32,32,128]{2,1,0:T(8,128)(2,1)S(1)} %add_convert_fusion), channel_id=1, replica_groups=mesh['zl'=4,'core'=2,'yh'=4,'yl'=2,'x'=4,'zh'=2] {'zl','yh','yl'}, dimensions={0} | all-to-all | bytes 524288 | tf_op jit(solution)/shard_map/all_to_all | solution.py:148
  106.1 0.1 reduce_sum.12
  106.1 11.0 %all_to_all.23 = bf16[8,32,128]{2,1,0:T(8,128)(2,1)S(1)} all-to-all(bf16[8,32,128]{2,1,0:T(8,128)(2,1)S(1)} %broadcast_in_dim.20), channel_id=1, replica_groups=mesh['zl'=4,'core'=2,'yh'=4,'yl'=2,'x'=4,'zh'=2] {'zl','core'}, dimensions={0} | all-to-all | bytes 131072 | tf_op jit(solution)/shard_map/all_to_all | solution.py:150
  117.1 2.8 %collective-permute-start.4 = (bf16[8,32,128]{2,1,0:T(8,128)(2,1)S(1)}, bf16[8,32,128]{2,1,0:T(8,128)(2,1)S(1)}, u32[]{:S(2)}, u32[]{:S(2)}) collective-permute-start(bf16[8,32,128]{2,1,0:T(8,128)(2,1)S(1)} %all_to_all.23), channel_id=1, source_target_pairs={{0,4},{64,2},{128,6},{192,0},{384,5},{448,3},{256,7},{320,1},{1,69... | collective-permute-start | bytes 196616 | tf_op jit(solution)/shard_map/ppermute | solution.py:151
  119.9 4.4 %collective-permute-done.4 = bf16[8,32,128]{2,1,0:T(8,128)(2,1)S(1)} collective-permute-done((bf16[8,32,128]{2,1,0:T(8,128)(2,1)S(1)}, bf16[8,32,128]{2,1,0:T(8,128)(2,1)S(1)}, u32[]{:S(2)}, u32[]{:S(2)}) %collective-permute-start.4) | collective-permute-done | bytes 65568 | tf_op jit(solution)/shard_map/ppermute | solution.py:151
  124.3 0.7 copy_bitcast_fusion
  (2 shorter events, 0.1 us)
Async XLA Ops:
  0.0 59.6 %copy-start.2 = (bf16[1,1,128,1024]{3,2,1,0:T(8,128)(2,1)S(1)}, bf16[1,1,128,1024]{3,2,1,0:T(8,128)(2,1)}, u32[]{:S(2)}) copy-start(bf16[1,1,128,1024]{3,2,1,0:T(8,128)(2,1)} %param.14) | copy-start | bytes 786436
  0.0 59.6 %copy-start.1 = (bf16[1,1,128,1024]{3,2,1,0:T(8,128)(2,1)S(1)}, bf16[1,1,128,1024]{3,2,1,0:T(8,128)(2,1)}, u32[]{:S(2)}) copy-start(bf16[1,1,128,1024]{3,2,1,0:T(8,128)(2,1)} %param.13) | copy-start | bytes 786436
  0.0 59.6 %copy-start.3 = (bf16[1,128]{1,0:T(2,128)(2,1)S(1)}, bf16[1,128]{1,0:T(2,128)(2,1)}, u32[]{:S(2)}) copy-start(bf16[1,128]{1,0:T(2,128)(2,1)} %gain.1) | copy-start | bytes 772
  0.0 59.6 %copy-start = (bf16[1,8192,128]{2,1,0:T(8,128)(2,1)S(1)}, bf16[1,8192,128]{2,1,0:T(8,128)(2,1)}, u32[]{:S(2)}) copy-start(bf16[1,8192,128]{2,1,0:T(8,128)(2,1)} %param.10) | copy-start | bytes 6291460
  39.6 20.1 %copy-start.4 = (bf16[48,8192]{1,0:T(8,128)(2,1)}, bf16[48,8192]{1,0:T(8,128)(2,1)S(1)}, u32[]{:S(2)}) copy-start(bf16[48,8192]{1,0:T(8,128)(2,1)S(1)} %reshape.335.same) | copy-start | bytes 2359300
  39.6 14.1 %collective-permute-start = (bf16[48,8192]{1,0:T(8,128)(2,1)S(1)}, bf16[48,8192]{1,0:T(8,128)(2,1)}, u32[]{:S(2)}, u32[]{:S(2)}) collective-permute-start(bf16[48,8192]{1,0:T(8,128)(2,1)S(1)} %reshape.335.same), channel_id=1, source_target_pairs={{8,0},{16,8},{24,16},{32,24},{40,32},{48,40},{56,48},{0,56},{120,6... | collective-permute-start | bytes 2359304 | tf_op jit(solution)/shard_map/ppermute | solution.py:121
  41.8 17.6 %collective-permute-start.1 = (bf16[48,8192]{1,0:T(8,128)(2,1)S(1)}, bf16[48,8192]{1,0:T(8,128)(2,1)}, u32[]{:S(2)}, u32[]{:S(2)}) collective-permute-start(bf16[48,8192]{1,0:T(8,128)(2,1)S(1)} %reshape.335.same), channel_id=1, source_target_pairs={{0,64},{64,0},{1,65},{65,1},{2,66},{66,2},{3,67},{67,3},{4,68},{68... | collective-permute-start | bytes 2359304 | tf_op jit(solution)/shard_map/ppermute | solution.py:122
  53.6 6.0 %collective-permute-start.2 = (bf16[48,8192]{1,0:T(8,128)(2,1)}, bf16[48,8192]{1,0:T(8,128)(2,1)}, u32[]{:S(2)}, u32[]{:S(2)}) collective-permute-start(bf16[48,8192]{1,0:T(8,128)(2,1)} %collective-permute-done.other), channel_id=1, source_target_pairs={{0,64},{64,0},{1,65},{65,1},{2,66},{66,2},{3,67},{67,3},{4,68},{68... | collective-permute-start | bytes 2359304 | tf_op jit(solution)/shard_map/ppermute | solution.py:123
  85.9 4.9 %collective-permute-start.3 = (bf16[32,32,128]{2,1,0:T(8,128)(2,1)S(1)}, bf16[32,32,128]{2,1,0:T(8,128)(2,1)S(1)}, u32[]{:S(2)}, u32[]{:S(2)}) collective-permute-start(bf16[32,32,128]{2,1,0:T(8,128)(2,1)S(1)} %get-tuple-element.12), channel_id=1, source_target_pairs={{0,64},{64,0},{1,65},{65,1},{2,66},{66,2},{3,67},{67,3},{4,68},{68... | collective-permute-start | bytes 786440 | tf_op jit(solution)/shard_map/ppermute | solution.py:146
  117.1 7.2 %collective-permute-start.4 = (bf16[8,32,128]{2,1,0:T(8,128)(2,1)S(1)}, bf16[8,32,128]{2,1,0:T(8,128)(2,1)S(1)}, u32[]{:S(2)}, u32[]{:S(2)}) collective-permute-start(bf16[8,32,128]{2,1,0:T(8,128)(2,1)S(1)} %all_to_all.23), channel_id=1, source_target_pairs={{0,4},{64,2},{128,6},{192,0},{384,5},{448,3},{256,7},{320,1},{1,69... | collective-permute-start | bytes 196616 | tf_op jit(solution)/shard_map/ppermute | solution.py:151

commit v3 on v2

--- a/solution.py
+++ b/solution.py
@@ -20,32 +20,14 @@
 BF16 = jnp.bfloat16
 
 
-def factors_kernel(
-    length, target, same, other, far_same, far_other, w_key, w_value, gain, query, grad, out, late, rows, sems
-):
+def factors_kernel(length, target, same, other, far_same, far_other, w_key, w_value, gain, query, grad, out):
     pieces = (same, other, far_same, far_other)
-
-    def load(step, i):
-        part = pl.ds(step * STEP, STEP)
-        return pltpu.make_async_copy(pieces[i].at[:, part], rows.at[pl.ds(48 * i, 48), part], sems.at[step, i])
-
-    def bring(step):
-        part = pl.ds(step * STEP, STEP)
-        return pltpu.make_async_copy(w_value.at[part, :], late.at[part, :], sems.at[step, 4])
-
-    steps = 8192 // STEP
-    for step in range(steps):
-        bring(step).start()
-        for i in range(4):
-            load(step, i).start()
     both = jnp.zeros((192, 256), F32)
-    for step in range(steps):
-        part = pl.ds(step * STEP, STEP)
-        for i in range(4):
-            load(step, i).wait()
-        bring(step).wait()
-        mats = jnp.concatenate([w_key[part, :], late[part, :]], axis=1)
-        both += jnp.dot(rows[:, part], mats, preferred_element_type=F32)
+    for start in range(0, 8192, STEP):
+        part = pl.ds(start, STEP)
+        rows = jnp.concatenate([piece[:, part] for piece in pieces], axis=0)
+        mats = jnp.concatenate([w_key[part, :], w_value[part, :]], axis=1)
+        both += jnp.dot(rows, mats, preferred_element_type=F32)
     kraw = both[:, :128]
     values = both[:, 128:].astype(BF16)
     scale_row = lax.rsqrt(jnp.mean(kraw * kraw, axis=1, keepdims=True) + EPS)
@@ -77,6 +59,12 @@
     out[...] = jnp.dot(onehot, fac, preferred_element_type=F32).astype(BF16)
 
 
+def bring_kernel(after, weights, out, sem):
+    copy = pltpu.make_async_copy(weights, out, sem)
+    copy.start()
+    copy.wait()
+
+
 def product_kernel(mine, parts, w_key, w_value, keep, give):
     total = jnp.zeros((BW, 256), F32)
     for c in range(8):
@@ -101,7 +89,7 @@
 def call(kernel, scalars, arrays, out_shape, limit, flops, kept=(), scratch=()):
     smem = pl.BlockSpec(memory_space=pltpu.SMEM)
     vmem = pl.BlockSpec(memory_space=pltpu.VMEM)
-    whole = pl.BlockSpec(memory_space=pltpu.HBM)
+    whole = pl.BlockSpec(memory_space=pl.ANY)
     return pl.pallas_call(
         kernel,
         in_specs=[smem] * len(scalars) + [whole if i in kept else vmem for i in range(len(arrays))],
@@ -128,15 +116,23 @@
     column = (((r // 3) % 4) * 2 + parity) * 3 + r % 3
     target = line * BW + offsets[0] + jnp.where(flips[0] == 1, GW - 1 - column, column)
     key_mat, value_mat = w_key[0], w_value[0]
-    placed, value_mat = call(
+    value_mat = call(
+        bring_kernel,
+        [],
+        [other, in_hbm(value_mat)],
+        jax.ShapeDtypeStruct((8192, 128), BF16),
+        1 << 20,
+        1 << 20,
+        kept=(0, 1),
+        scratch=[pltpu.SemaphoreType.DMA],
+    )
+    placed = call(
         factors_kernel,
         [lengths],
-        [target[None], *map(in_hbm, rows), key_mat, in_hbm(value_mat), key_gain, queries[0, 0], grad_out[0, 0]],
-        (jax.ShapeDtypeStruct((256, 256), BF16), jax.ShapeDtypeStruct((8192, 128), BF16)),
+        [target[None], *rows, key_mat, value_mat, key_gain, queries[0, 0], grad_out[0, 0]],
+        jax.ShapeDtypeStruct((256, 256), BF16),
         12 << 20,
         1 << 30,
-        kept=(1, 2, 3, 4, 6),
-        scratch=[pltpu.VMEM((192, 8192), BF16), pltpu.SemaphoreType.DMA((8192 // STEP, 5))],
     )
     parts = lax.all_to_all(placed.reshape(8, BW, 256), COPY, 0, 0)
     block = jax.ShapeDtypeStruct((32, BW, 128), BF16)

time: 126 us -> 124 us (0.984)
    pallas_call x2 -> x3, Pallas kernels: 7.18 us -> 7.02 us  [call(): pl.pallas_call(kernel, in_specs=[smem] * len(scalars) + [whole if i in ke...]
  transfers between devices with their start and end apart: 5 -> 5, of which waited for: 4 -> 3; matrix products, arithmetic and copies ran while one was open for 0% -> 0% of each run, Pallas kernels for 0% -> 1%
where the time goes in v3:
time: 124 us; the launch traced here: 123 us
  blocking collectives  82.1 us (66%)
  starting transfers between devices  15.6 us (13%)
  waiting for transfers between devices  13.7 us (11%)
  Pallas kernels  7.02 us (6%)
  between operations  2.08 us (2%)
  local copies, waits for them, and re-layouts  1.85 us (1%)
    all_to_all x1, blocking collectives, on_device(): same = lax.all_to_all(spread, ('zl', 'yh'), 0, 0).reshape(48, 8192)  36.8 us
    all_to_all x1, blocking collectives, on_device(): parts = lax.all_to_all(placed.reshape(8, BW, 256), COPY, 0, 0)  19 us
    all_to_all x1, blocking collectives, on_device(): pieces = lax.all_to_all(pair, ('zl',) + TENSOR, 0, 0)  15.2 us
    all_to_all x1, blocking collectives, on_device(): lax.all_to_all(jnp.broadcast_to(total[None], (8, BW, 128)), SECTION, 0, 0)  11 us
    ppermute x1, waiting for transfers between devices, on_device(): other = lax.ppermute(same, ('core',) + TENSOR, walk)  8.18 us
    pallas_call x3, Pallas kernels, call(): pl.pallas_call(kernel, in_specs=[smem] * len(scalars) + [whole if i in ke...  7.02 us
    ppermute x1, waiting for transfers between devices, on_device(): out = lax.ppermute(wide, SECTION + COPY, turn())  4.39 us
    ppermute x1, starting transfers between devices, on_device(): far_other = lax.ppermute(other, 'core', SWAP)  3.76 us
  transfers between devices with their start and end apart: 5, of which 3 were waited for; matrix products, arithmetic and copies ran while one was open for 0% of the time, Pallas kernels for 1%

profile of v3, /device:TPU:1, one launch (start us, length us, event | category | flops | bytes accessed | tf_op | source)
XLA Modules:
  0.0 123.2 jit_solution(3209513676532647510)
XLA Ops:
  0.0 0.9 broadcast_in_dim.18
  0.9 0.1 broadcast_in_dim.19
  1.0 36.8 %all_to_all.20 = bf16[16,24,1024]{2,1,0:T(8,128)(2,1)S(1)} all-to-all(bf16[16,24,1024]{2,1,0:T(8,128)(2,1)S(1)} %broadcast_in_dim.19), channel_id=1, replica_groups=mesh['zl'=4,'core'=2,'yh'=4,'yl'=2,'x'=4,'zh'=2] {'zl','yh'}, dimensions={0} | all-to-all | bytes 1572864 | tf_op jit(solution)/shard_map/all_to_all | solution.py:107
  37.8 0.4 reshape.335.same
  38.2 2.2 %collective-permute-start = (bf16[48,8192]{1,0:T(8,128)(2,1)S(1)}, bf16[48,8192]{1,0:T(8,128)(2,1)S(1)}, u32[]{:S(2)}, u32[]{:S(2)}) collective-permute-start(bf16[48,8192]{1,0:T(8,128)(2,1)S(1)} %reshape.335.same), channel_id=1, source_target_pairs={{8,0},{16,8},{24,16},{32,24},{40,32},{48,40},{56,48},{0,56},{120,6... | collective-permute-start | bytes 2359304 | tf_op jit(solution)/shard_map/ppermute | solution.py:109
  40.4 3.5 %collective-permute-start.1 = (bf16[48,8192]{1,0:T(8,128)(2,1)S(1)}, bf16[48,8192]{1,0:T(8,128)(2,1)S(1)}, u32[]{:S(2)}, u32[]{:S(2)}) collective-permute-start(bf16[48,8192]{1,0:T(8,128)(2,1)S(1)} %reshape.335.same), channel_id=1, source_target_pairs={{0,64},{64,0},{1,65},{65,1},{2,66},{66,2},{3,67},{67,3},{4,68},{68... | collective-permute-start | bytes 2359304 | tf_op jit(solution)/shard_map/ppermute | solution.py:110
  44.0 8.2 %collective-permute-done.after.other = bf16[48,8192]{1,0:T(8,128)(2,1)S(1)} collective-permute-done((bf16[48,8192]{1,0:T(8,128)(2,1)S(1)}, bf16[48,8192]{1,0:T(8,128)(2,1)S(1)}, u32[]{:S(2)}, u32[]{:S(2)}) %collective-permute-start) | collective-permute-done | bytes 786464 | tf_op jit(solution)/shard_map/ppermute | solution.py:109
  52.2 3.8 %collective-permute-start.2 = (bf16[48,8192]{1,0:T(8,128)(2,1)S(1)}, bf16[48,8192]{1,0:T(8,128)(2,1)S(1)}, u32[]{:S(2)}, u32[]{:S(2)}) collective-permute-start(bf16[48,8192]{1,0:T(8,128)(2,1)S(1)} %collective-permute-done.after.other), channel_id=1, source_target_pairs={{0,64},{64,0},{1,65},{65,1},{2,66},{66,2},{3,67},{67,3},{4,68},{68... | collective-permute-start | bytes 2359304 | tf_op jit(solution)/shard_map/ppermute | solution.py:111
  57.9 0.0 copy-start
  57.9 0.0 copy-start.1
  57.9 0.0 copy-start.2
  58.0 0.0 copy-start.3
  58.0 1.8 %shard_map.91.w_value = bf16[8192,128]{1,0:T(8,128)(2,1)S(1)} custom-call(bf16[48,8192]{1,0:T(8,128)(2,1)S(1)} %collective-permute-done.after.other, bf16[8192,128]{1,0:T(8,128)(2,1)} %bitcast.20), custom_call_target="tpu_custom_call" | custom-call | flops 1048576 | bytes 8388608 | tf_op jit(solution)/shard_map/pallas_call | solution.py:93
  59.7 0.0 collective-permute-done.1.far_same
  59.7 0.0 collective-permute-done.2.far_other
  59.7 0.4 copy-done
  60.1 0.0 copy-done.1
  60.1 0.1 copy-done.2
  60.2 0.0 copy-done.3
  60.2 3.9 %shard_map.92 = bf16[256,256]{1,0:T(8,128)(2,1)S(1)} custom-call(s32[1]{0:T(128)S(6)} %copy.15.length, s32[1,192]{1,0:T(1,128)S(1)} %fusion.3.target, bf16[48,8192]{1,0:T(8,128)(2,1)S(1)} %reshape.335.same, bf16[48,8192]{1,0:T(8,128)(2,1)S(1)} %collective-permute-done.after.other, bf16[48,8192]{1,0:T(8,128)(2,1)S(1)} %collective-permute-done.1.far_same, ...), custom_call_target="tpu_custom_call" | custom-call | flops 1073741824 | bytes 8388608 | tf_op jit(solution)/shard_map/pallas_call | solution.py:93
  64.1 19.0 %all_to_all.21.parts = bf16[8,32,256]{2,1,0:T(8,128)(2,1)S(1)} all-to-all(bf16[8,32,256]{2,1,0:T(8,128)(2,1)S(1)} %bitcast.17), channel_id=1, replica_groups=mesh['zl'=4,'core'=2,'yh'=4,'yl'=2,'x'=4,'zh'=2] {'x','zh'}, dimensions={0} | all-to-all | bytes 262144 | tf_op jit(solution)/shard_map/all_to_all | solution.py:137
  83.2 1.4 %shard_map.93 = (bf16[32,32,128]{2,1,0:T(8,128)(2,1)S(1)}, bf16[32,32,128]{2,1,0:T(8,128)(2,1)S(1)}) custom-call(s32[1]{0:T(128)} %bitcast.mine, bf16[8,32,256]{2,1,0:T(8,128)(2,1)S(1)} %all_to_all.21.parts, bf16[8192,128]{1,0:T(8,128)(2,1)S(1)} %bitcast.16, bf16[8192,128]{1,0:T(8,128)(2,1)S(1)} %shard_map.91.w_value), custom_call_target="tpu_custom_call" | custom-call | flops 134217728 | bytes 8388608 | tf_op jit(solution)/shard_map/pallas_call | solution.py:93
  84.5 3.4 %collective-permute-start.3 = (bf16[32,32,128]{2,1,0:T(8,128)(2,1)S(1)}, bf16[32,32,128]{2,1,0:T(8,128)(2,1)S(1)}, u32[]{:S(2)}, u32[]{:S(2)}) collective-permute-start(bf16[32,32,128]{2,1,0:T(8,128)(2,1)S(1)} %get-tuple-element.8), channel_id=1, source_target_pairs={{0,64},{64,0},{1,65},{65,1},{2,66},{66,2},{3,67},{67,3},{4,68},{68... | collective-permute-start | bytes 786440 | tf_op jit(solution)/shard_map/ppermute | solution.py:142
  87.9 1.1 collective-permute-done.3
  89.0 0.1 add_convert_fusion
  89.1 15.2 %all_to_all.22 = bf16[32,32,128]{2,1,0:T(8,128)(2,1)S(1)} all-to-all(bf16[32,32,128]{2,1,0:T(8,128)(2,1)S(1)} %add_convert_fusion), channel_id=1, replica_groups=mesh['zl'=4,'core'=2,'yh'=4,'yl'=2,'x'=4,'zh'=2] {'zl','yh','yl'}, dimensions={0} | all-to-all | bytes 524288 | tf_op jit(solution)/shard_map/all_to_all | solution.py:144
  104.3 0.1 reduce_sum.12
  104.4 11.0 %all_to_all.23 = bf16[8,32,128]{2,1,0:T(8,128)(2,1)S(1)} all-to-all(bf16[8,32,128]{2,1,0:T(8,128)(2,1)S(1)} %broadcast_in_dim.20), channel_id=1, replica_groups=mesh['zl'=4,'core'=2,'yh'=4,'yl'=2,'x'=4,'zh'=2] {'zl','core'}, dimensions={0} | all-to-all | bytes 131072 | tf_op jit(solution)/shard_map/all_to_all | solution.py:146
  115.4 2.8 %collective-permute-start.4 = (bf16[8,32,128]{2,1,0:T(8,128)(2,1)S(1)}, bf16[8,32,128]{2,1,0:T(8,128)(2,1)S(1)}, u32[]{:S(2)}, u32[]{:S(2)}) collective-permute-start(bf16[8,32,128]{2,1,0:T(8,128)(2,1)S(1)} %all_to_all.23), channel_id=1, source_target_pairs={{0,4},{64,2},{128,6},{192,0},{384,5},{448,3},{256,7},{320,1},{1,69... | collective-permute-start | bytes 196616 | tf_op jit(solution)/shard_map/ppermute | solution.py:147
  118.1 4.4 %collective-permute-done.4 = bf16[8,32,128]{2,1,0:T(8,128)(2,1)S(1)} collective-permute-done((bf16[8,32,128]{2,1,0:T(8,128)(2,1)S(1)}, bf16[8,32,128]{2,1,0:T(8,128)(2,1)S(1)}, u32[]{:S(2)}, u32[]{:S(2)}) %collective-permute-start.4) | collective-permute-done | bytes 65568 | tf_op jit(solution)/shard_map/ppermute | solution.py:147
  122.5 0.7 copy_bitcast_fusion
  (2 shorter events, 0.1 us)
Async XLA Ops:
  38.2 13.9 %collective-permute-start = (bf16[48,8192]{1,0:T(8,128)(2,1)S(1)}, bf16[48,8192]{1,0:T(8,128)(2,1)S(1)}, u32[]{:S(2)}, u32[]{:S(2)}) collective-permute-start(bf16[48,8192]{1,0:T(8,128)(2,1)S(1)} %reshape.335.same), channel_id=1, source_target_pairs={{8,0},{16,8},{24,16},{32,24},{40,32},{48,40},{56,48},{0,56},{120,6... | collective-permute-start | bytes 2359304 | tf_op jit(solution)/shard_map/ppermute | solution.py:109
  40.4 19.3 %collective-permute-start.1 = (bf16[48,8192]{1,0:T(8,128)(2,1)S(1)}, bf16[48,8192]{1,0:T(8,128)(2,1)S(1)}, u32[]{:S(2)}, u32[]{:S(2)}) collective-permute-start(bf16[48,8192]{1,0:T(8,128)(2,1)S(1)} %reshape.335.same), channel_id=1, source_target_pairs={{0,64},{64,0},{1,65},{65,1},{2,66},{66,2},{3,67},{67,3},{4,68},{68... | collective-permute-start | bytes 2359304 | tf_op jit(solution)/shard_map/ppermute | solution.py:110
  52.2 7.6 %collective-permute-start.2 = (bf16[48,8192]{1,0:T(8,128)(2,1)S(1)}, bf16[48,8192]{1,0:T(8,128)(2,1)S(1)}, u32[]{:S(2)}, u32[]{:S(2)}) collective-permute-start(bf16[48,8192]{1,0:T(8,128)(2,1)S(1)} %collective-permute-done.after.other), channel_id=1, source_target_pairs={{0,64},{64,0},{1,65},{65,1},{2,66},{66,2},{3,67},{67,3},{4,68},{68... | collective-permute-start | bytes 2359304 | tf_op jit(solution)/shard_map/ppermute | solution.py:111
  57.9 2.2 %copy-start = (bf16[1,8192,128]{2,1,0:T(8,128)(2,1)S(1)}, bf16[1,8192,128]{2,1,0:T(8,128)(2,1)}, u32[]{:S(2)}) copy-start(bf16[1,8192,128]{2,1,0:T(8,128)(2,1)} %param.10) | copy-start | bytes 6291460
  57.9 2.2 %copy-start.1 = (bf16[1,1,128,1024]{3,2,1,0:T(8,128)(2,1)S(1)}, bf16[1,1,128,1024]{3,2,1,0:T(8,128)(2,1)}, u32[]{:S(2)}) copy-start(bf16[1,1,128,1024]{3,2,1,0:T(8,128)(2,1)} %param.13) | copy-start | bytes 786436
  57.9 2.3 %copy-start.2 = (bf16[1,1,128,1024]{3,2,1,0:T(8,128)(2,1)S(1)}, bf16[1,1,128,1024]{3,2,1,0:T(8,128)(2,1)}, u32[]{:S(2)}) copy-start(bf16[1,1,128,1024]{3,2,1,0:T(8,128)(2,1)} %param.14) | copy-start | bytes 786436
  58.0 2.3 %copy-start.3 = (bf16[1,128]{1,0:T(2,128)(2,1)S(1)}, bf16[1,128]{1,0:T(2,128)(2,1)}, u32[]{:S(2)}) copy-start(bf16[1,128]{1,0:T(2,128)(2,1)} %gain.1) | copy-start | bytes 772
  84.5 4.5 %collective-permute-start.3 = (bf16[32,32,128]{2,1,0:T(8,128)(2,1)S(1)}, bf16[32,32,128]{2,1,0:T(8,128)(2,1)S(1)}, u32[]{:S(2)}, u32[]{:S(2)}) collective-permute-start(bf16[32,32,128]{2,1,0:T(8,128)(2,1)S(1)} %get-tuple-element.8), channel_id=1, source_target_pairs={{0,64},{64,0},{1,65},{65,1},{2,66},{66,2},{3,67},{67,3},{4,68},{68... | collective-permute-start | bytes 786440 | tf_op jit(solution)/shard_map/ppermute | solution.py:142
  115.4 7.2 %collective-permute-start.4 = (bf16[8,32,128]{2,1,0:T(8,128)(2,1)S(1)}, bf16[8,32,128]{2,1,0:T(8,128)(2,1)S(1)}, u32[]{:S(2)}, u32[]{:S(2)}) collective-permute-start(bf16[8,32,128]{2,1,0:T(8,128)(2,1)S(1)} %all_to_all.23), channel_id=1, source_target_pairs={{0,4},{64,2},{128,6},{192,0},{384,5},{448,3},{256,7},{320,1},{1,69... | collective-permute-start | bytes 196616 | tf_op jit(solution)/shard_map/ppermute | solution.py:147

commit v4 on v3

--- a/solution.py
+++ b/solution.py
@@ -108,13 +108,14 @@
     walk = [(k * 8 + (y + 1 - 2 * k) % 8, k * 8 + y) for k in range(2) for y in range(8)]
     other = lax.ppermute(same, ("core",) + TENSOR, walk)
     far_same = lax.ppermute(same, "core", SWAP)
-    far_other = lax.ppermute(other, "core", SWAP)
-    rows = [same, other, far_same, far_other]
     r = jnp.arange(192, dtype=jnp.int32)
     line = ((r // 12) % 4) * 2 + (core + r // 96) % 2
     parity = (lax.axis_index("yl") + (r // 48) % 2) % 2
     column = (((r // 3) % 4) * 2 + parity) * 3 + r % 3
     target = line * BW + offsets[0] + jnp.where(flips[0] == 1, GW - 1 - column, column)
+    other, target, lengths = lax.optimization_barrier((other, target, lengths))
+    far_other = lax.ppermute(other, "core", SWAP)
+    rows = [same, other, far_same, far_other]
     key_mat, value_mat = w_key[0], w_value[0]
     value_mat = call(
         bring_kernel,

time: 124 us -> 123 us (level)
  waiting for transfers between devices: 13.7 us -> 12.4 us
    ppermute x1, waiting for transfers between devices: 8.18 us -> 6.84 us  [on_device(): other = lax.ppermute(same, ('core',) + TENSOR, walk)]
where the time goes in v4:
time: 123 us; the launch traced here: 122 us
  blocking collectives  82.1 us (67%)
  starting transfers between devices  15.6 us (13%)
  waiting for transfers between devices  12.4 us (10%)
  Pallas kernels  7.04 us (6%)
  between operations  2.08 us (2%)
  local copies, waits for them, and re-layouts  1.85 us (2%)
    all_to_all x1, blocking collectives, on_device(): same = lax.all_to_all(spread, ('zl', 'yh'), 0, 0).reshape(48, 8192)  36.8 us
    all_to_all x1, blocking collectives, on_device(): parts = lax.all_to_all(placed.reshape(8, BW, 256), COPY, 0, 0)  19 us
    all_to_all x1, blocking collectives, on_device(): pieces = lax.all_to_all(pair, ('zl',) + TENSOR, 0, 0)  15.2 us
    all_to_all x1, blocking collectives, on_device(): lax.all_to_all(jnp.broadcast_to(total[None], (8, BW, 128)), SECTION, 0, 0)  11 us
    pallas_call x3, Pallas kernels, call(): pl.pallas_call(kernel, in_specs=[smem] * len(scalars) + [whole if i in ke...  7.04 us
    ppermute x1, waiting for transfers between devices, on_device(): other = lax.ppermute(same, ('core',) + TENSOR, walk)  6.84 us
    ppermute x1, waiting for transfers between devices, on_device(): out = lax.ppermute(wide, SECTION + COPY, turn())  4.39 us
    ppermute x1, starting transfers between devices, on_device(): far_other = lax.ppermute(other, 'core', SWAP)  3.76 us
  transfers between devices with their start and end apart: 5, of which 3 were waited for; matrix products, arithmetic and copies ran while one was open for 0% of the time, Pallas kernels for 1%

profile of v4, /device:TPU:1, one launch (start us, length us, event | category | flops | bytes accessed | tf_op | source)
XLA Modules:
  0.0 121.9 jit_solution(11317923207838589605)
XLA Ops:
  0.0 0.9 broadcast_in_dim.20
  0.9 0.1 broadcast_in_dim.21
  1.0 36.8 %all_to_all.20 = bf16[16,24,1024]{2,1,0:T(8,128)(2,1)S(1)} all-to-all(bf16[16,24,1024]{2,1,0:T(8,128)(2,1)S(1)} %broadcast_in_dim.21), channel_id=1, replica_groups=mesh['zl'=4,'core'=2,'yh'=4,'yl'=2,'x'=4,'zh'=2] {'zl','yh'}, dimensions={0} | all-to-all | bytes 1572864 | tf_op jit(solution)/shard_map/all_to_all | solution.py:107
  37.8 0.4 reshape.13.same
  38.2 2.2 %collective-permute-start = (bf16[48,8192]{1,0:T(8,128)(2,1)S(1)}, bf16[48,8192]{1,0:T(8,128)(2,1)S(1)}, u32[]{:S(2)}, u32[]{:S(2)}) collective-permute-start(bf16[48,8192]{1,0:T(8,128)(2,1)S(1)} %reshape.13.same), channel_id=1, source_target_pairs={{8,0},{16,8},{24,16},{32,24},{40,32},{48,40},{56,48},{0,56},{120,6... | collective-permute-start | bytes 2359304 | tf_op jit(solution)/shard_map/ppermute | solution.py:109
  41.8 3.5 %collective-permute-start.1 = (bf16[48,8192]{1,0:T(8,128)(2,1)S(1)}, bf16[48,8192]{1,0:T(8,128)(2,1)S(1)}, u32[]{:S(2)}, u32[]{:S(2)}) collective-permute-start(bf16[48,8192]{1,0:T(8,128)(2,1)S(1)} %reshape.13.same), channel_id=1, source_target_pairs={{0,64},{64,0},{1,65},{65,1},{2,66},{66,2},{3,67},{67,3},{4,68},{68... | collective-permute-start | bytes 2359304 | tf_op jit(solution)/shard_map/ppermute | solution.py:110
  45.3 6.8 %collective-permute-done.after.other = bf16[48,8192]{1,0:T(8,128)(2,1)S(1)} collective-permute-done((bf16[48,8192]{1,0:T(8,128)(2,1)S(1)}, bf16[48,8192]{1,0:T(8,128)(2,1)S(1)}, u32[]{:S(2)}, u32[]{:S(2)}) %collective-permute-start) | collective-permute-done | bytes 786464 | tf_op jit(solution)/shard_map/ppermute | solution.py:109
  52.2 3.8 %collective-permute-start.2 = (bf16[48,8192]{1,0:T(8,128)(2,1)S(1)}, bf16[48,8192]{1,0:T(8,128)(2,1)S(1)}, u32[]{:S(2)}, u32[]{:S(2)}) collective-permute-start(bf16[48,8192]{1,0:T(8,128)(2,1)S(1)} %collective-permute-done.after.other), channel_id=1, source_target_pairs={{0,64},{64,0},{1,65},{65,1},{2,66},{66,2},{3,67},{67,3},{4,68},{68... | collective-permute-start | bytes 2359304 | tf_op jit(solution)/shard_map/ppermute | solution.py:117
  56.6 0.0 copy-start
  56.6 0.0 copy-start.1
  56.6 0.0 copy-start.2
  56.6 0.0 copy-start.3
  56.6 1.8 %shard_map.91.w_value = bf16[8192,128]{1,0:T(8,128)(2,1)S(1)} custom-call(bf16[48,8192]{1,0:T(8,128)(2,1)S(1)} %collective-permute-done.after.other, bf16[8192,128]{1,0:T(8,128)(2,1)} %bitcast.22), custom_call_target="tpu_custom_call" | custom-call | flops 1048576 | bytes 8388608 | tf_op jit(solution)/shard_map/pallas_call | solution.py:93
  58.4 0.0 collective-permute-done.1.far_same
  58.4 0.0 collective-permute-done.2.far_other
  58.4 0.4 copy-done
  58.8 0.0 copy-done.1
  58.8 0.1 copy-done.2
  58.9 0.0 copy-done.3
  58.9 3.9 %shard_map.92 = bf16[256,256]{1,0:T(8,128)(2,1)S(1)} custom-call(s32[1]{0:T(128)S(6)} %copy.15.length, s32[1,192]{1,0:T(1,128)S(1)} %bitcast.21, bf16[48,8192]{1,0:T(8,128)(2,1)S(1)} %reshape.13.same, bf16[48,8192]{1,0:T(8,128)(2,1)S(1)} %collective-permute-done.after.other, bf16[48,8192]{1,0:T(8,128)(2,1)S(1)} %collective-permute-done.1.far_same, ...), custom_call_target="tpu_custom_call" | custom-call | flops 1073741824 | bytes 8388608 | tf_op jit(solution)/shard_map/pallas_call | solution.py:93
  62.8 19.0 %all_to_all.21.parts = bf16[8,32,256]{2,1,0:T(8,128)(2,1)S(1)} all-to-all(bf16[8,32,256]{2,1,0:T(8,128)(2,1)S(1)} %bitcast.18), channel_id=1, replica_groups=mesh['zl'=4,'core'=2,'yh'=4,'yl'=2,'x'=4,'zh'=2] {'x','zh'}, dimensions={0} | all-to-all | bytes 262144 | tf_op jit(solution)/shard_map/all_to_all | solution.py:138
  81.8 1.4 %shard_map.93 = (bf16[32,32,128]{2,1,0:T(8,128)(2,1)S(1)}, bf16[32,32,128]{2,1,0:T(8,128)(2,1)S(1)}) custom-call(s32[1]{0:T(128)} %bitcast.mine, bf16[8,32,256]{2,1,0:T(8,128)(2,1)S(1)} %all_to_all.21.parts, bf16[8192,128]{1,0:T(8,128)(2,1)S(1)} %bitcast.17, bf16[8192,128]{1,0:T(8,128)(2,1)S(1)} %shard_map.91.w_value), custom_call_target="tpu_custom_call" | custom-call | flops 134217728 | bytes 8388608 | tf_op jit(solution)/shard_map/pallas_call | solution.py:93
  83.2 3.4 %collective-permute-start.3 = (bf16[32,32,128]{2,1,0:T(8,128)(2,1)S(1)}, bf16[32,32,128]{2,1,0:T(8,128)(2,1)S(1)}, u32[]{:S(2)}, u32[]{:S(2)}) collective-permute-start(bf16[32,32,128]{2,1,0:T(8,128)(2,1)S(1)} %get-tuple-element.14), channel_id=1, source_target_pairs={{0,64},{64,0},{1,65},{65,1},{2,66},{66,2},{3,67},{67,3},{4,68},{68... | collective-permute-start | bytes 786440 | tf_op jit(solution)/shard_map/ppermute | solution.py:143
  86.6 1.1 collective-permute-done.3
  87.7 0.1 add_convert_fusion
  87.8 15.2 %all_to_all.22 = bf16[32,32,128]{2,1,0:T(8,128)(2,1)S(1)} all-to-all(bf16[32,32,128]{2,1,0:T(8,128)(2,1)S(1)} %add_convert_fusion), channel_id=1, replica_groups=mesh['zl'=4,'core'=2,'yh'=4,'yl'=2,'x'=4,'zh'=2] {'zl','yh','yl'}, dimensions={0} | all-to-all | bytes 524288 | tf_op jit(solution)/shard_map/all_to_all | solution.py:145
  103.0 0.1 reduce_sum.12
  103.1 11.0 %all_to_all.23 = bf16[8,32,128]{2,1,0:T(8,128)(2,1)S(1)} all-to-all(bf16[8,32,128]{2,1,0:T(8,128)(2,1)S(1)} %broadcast_in_dim.23), channel_id=1, replica_groups=mesh['zl'=4,'core'=2,'yh'=4,'yl'=2,'x'=4,'zh'=2] {'zl','core'}, dimensions={0} | all-to-all | bytes 131072 | tf_op jit(solution)/shard_map/all_to_all | solution.py:147
  114.0 2.8 %collective-permute-start.4 = (bf16[8,32,128]{2,1,0:T(8,128)(2,1)S(1)}, bf16[8,32,128]{2,1,0:T(8,128)(2,1)S(1)}, u32[]{:S(2)}, u32[]{:S(2)}) collective-permute-start(bf16[8,32,128]{2,1,0:T(8,128)(2,1)S(1)} %all_to_all.23), channel_id=1, source_target_pairs={{0,4},{64,2},{128,6},{192,0},{384,5},{448,3},{256,7},{320,1},{1,69... | collective-permute-start | bytes 196616 | tf_op jit(solution)/shard_map/ppermute | solution.py:148
  116.8 4.4 %collective-permute-done.4 = bf16[8,32,128]{2,1,0:T(8,128)(2,1)S(1)} collective-permute-done((bf16[8,32,128]{2,1,0:T(8,128)(2,1)S(1)}, bf16[8,32,128]{2,1,0:T(8,128)(2,1)S(1)}, u32[]{:S(2)}, u32[]{:S(2)}) %collective-permute-start.4) | collective-permute-done | bytes 65568 | tf_op jit(solution)/shard_map/ppermute | solution.py:148
  121.2 0.7 copy_bitcast_fusion
  (2 shorter events, 0.0 us)
Async XLA Ops:
  38.2 13.9 %collective-permute-start = (bf16[48,8192]{1,0:T(8,128)(2,1)S(1)}, bf16[48,8192]{1,0:T(8,128)(2,1)S(1)}, u32[]{:S(2)}, u32[]{:S(2)}) collective-permute-start(bf16[48,8192]{1,0:T(8,128)(2,1)S(1)} %reshape.13.same), channel_id=1, source_target_pairs={{8,0},{16,8},{24,16},{32,24},{40,32},{48,40},{56,48},{0,56},{120,6... | collective-permute-start | bytes 2359304 | tf_op jit(solution)/shard_map/ppermute | solution.py:109
  41.8 16.6 %collective-permute-start.1 = (bf16[48,8192]{1,0:T(8,128)(2,1)S(1)}, bf16[48,8192]{1,0:T(8,128)(2,1)S(1)}, u32[]{:S(2)}, u32[]{:S(2)}) collective-permute-start(bf16[48,8192]{1,0:T(8,128)(2,1)S(1)} %reshape.13.same), channel_id=1, source_target_pairs={{0,64},{64,0},{1,65},{65,1},{2,66},{66,2},{3,67},{67,3},{4,68},{68... | collective-permute-start | bytes 2359304 | tf_op jit(solution)/shard_map/ppermute | solution.py:110
  52.2 6.2 %collective-permute-start.2 = (bf16[48,8192]{1,0:T(8,128)(2,1)S(1)}, bf16[48,8192]{1,0:T(8,128)(2,1)S(1)}, u32[]{:S(2)}, u32[]{:S(2)}) collective-permute-start(bf16[48,8192]{1,0:T(8,128)(2,1)S(1)} %collective-permute-done.after.other), channel_id=1, source_target_pairs={{0,64},{64,0},{1,65},{65,1},{2,66},{66,2},{3,67},{67,3},{4,68},{68... | collective-permute-start | bytes 2359304 | tf_op jit(solution)/shard_map/ppermute | solution.py:117
  56.6 2.2 %copy-start = (bf16[1,8192,128]{2,1,0:T(8,128)(2,1)S(1)}, bf16[1,8192,128]{2,1,0:T(8,128)(2,1)}, u32[]{:S(2)}) copy-start(bf16[1,8192,128]{2,1,0:T(8,128)(2,1)} %param.10) | copy-start | bytes 6291460
  56.6 2.2 %copy-start.1 = (bf16[1,1,128,1024]{3,2,1,0:T(8,128)(2,1)S(1)}, bf16[1,1,128,1024]{3,2,1,0:T(8,128)(2,1)}, u32[]{:S(2)}) copy-start(bf16[1,1,128,1024]{3,2,1,0:T(8,128)(2,1)} %param.13) | copy-start | bytes 786436
  56.6 2.3 %copy-start.2 = (bf16[1,1,128,1024]{3,2,1,0:T(8,128)(2,1)S(1)}, bf16[1,1,128,1024]{3,2,1,0:T(8,128)(2,1)}, u32[]{:S(2)}) copy-start(bf16[1,1,128,1024]{3,2,1,0:T(8,128)(2,1)} %param.14) | copy-start | bytes 786436
  56.6 2.3 %copy-start.3 = (bf16[1,128]{1,0:T(2,128)(2,1)S(1)}, bf16[1,128]{1,0:T(2,128)(2,1)}, u32[]{:S(2)}) copy-start(bf16[1,128]{1,0:T(2,128)(2,1)} %gain.1) | copy-start | bytes 772
  83.2 4.5 %collective-permute-start.3 = (bf16[32,32,128]{2,1,0:T(8,128)(2,1)S(1)}, bf16[32,32,128]{2,1,0:T(8,128)(2,1)S(1)}, u32[]{:S(2)}, u32[]{:S(2)}) collective-permute-start(bf16[32,32,128]{2,1,0:T(8,128)(2,1)S(1)} %get-tuple-element.14), channel_id=1, source_target_pairs={{0,64},{64,0},{1,65},{65,1},{2,66},{66,2},{3,67},{67,3},{4,68},{68... | collective-permute-start | bytes 786440 | tf_op jit(solution)/shard_map/ppermute | solution.py:143
  114.0 7.2 %collective-permute-start.4 = (bf16[8,32,128]{2,1,0:T(8,128)(2,1)S(1)}, bf16[8,32,128]{2,1,0:T(8,128)(2,1)S(1)}, u32[]{:S(2)}, u32[]{:S(2)}) collective-permute-start(bf16[8,32,128]{2,1,0:T(8,128)(2,1)S(1)} %all_to_all.23), channel_id=1, source_target_pairs={{0,4},{64,2},{128,6},{192,0},{384,5},{448,3},{256,7},{320,1},{1,69... | collective-permute-start | bytes 196616 | tf_op jit(solution)/shard_map/ppermute | solution.py:148
